TPU v7x, 256 devices: a whole 4x4x8 slice. The times are simulated.
256 devices in a mesh: seq: 32 (over x, y, z_hi), head: 8 (over z_lo, core).
Axes of the slice: x: 4, y: 4, z: 8 (z_hi: 2, z_lo: 4; z = z_hi * 4 + z_lo), core: 2. Of those that a mesh axis runs over, the one named last changes fastest.
Arguments:
- queries: bfloat16 [16384, 3072], P(('seq', 'head')), may hold values from -8 to 8
- key_vectors: bfloat16 [16384, 3072], P(('seq', 'head')), may hold values from -8 to 8
- value_vectors: bfloat16 [16384, 3072], P(('seq', 'head')), may hold values from -6 to 6
- block_mask: int32 [24, 128, 128], P('head'), may hold values from 0 to 1, as said below
- layout: int32 [128], replicated, may hold values from 0 to 127, as said below
Outputs:
- attended: bfloat16 [16384, 3072], P(('seq', 'head'))
Inputs may be any that keep to these rules, and one draw needn't show every extreme that they name: block_mask[h, c, c] = 1 for every head h and block c. `layout`: a permutation of the block numbers.
All inputs are finite; a program needn't handle non-finite values.
Results may differ from a plain program's by a relative error of at most 0.0035.
Values may be sent and summed in bfloat16 or wider, within the bound.
A program may use at most 128 MiB of HBM per device.

v0:
```python
import math

import jax
import jax.numpy as jnp
from jax import lax
from jax.sharding import PartitionSpec as P

HEAD_DIM = 128
BLOCK = 128


def in_one_piece(arrays, axis, dim, along):
    both = jnp.concatenate(arrays, axis=along)
    filled, at, outs = (lax.all_gather(both, axis, axis=dim, tiled=True), 0, [])
    for a in arrays:
        outs.append(lax.slice_in_dim(filled, at, at + a.shape[along], axis=along))
        at += a.shape[along]
    return tuple(outs)


def per_device(queries, key_vectors, value_vectors, block_mask, layout):
    seq_count = lax.axis_size("seq")
    seq_index = lax.axis_index("seq")
    width = queries.shape[1]
    head_count = lax.axis_size("head")
    part_width = width // head_count
    head_width = HEAD_DIM
    heads_here = part_width // head_width
    block_rows = BLOCK
    scale = 1.0 / math.sqrt(head_width)
    local_queries, local_keys, local_values = (
        lax.all_to_all(queries, "head", split_axis=1, concat_axis=0, tiled=True),
        lax.all_to_all(key_vectors, "head", split_axis=1, concat_axis=0, tiled=True),
        lax.all_to_all(value_vectors, "head", split_axis=1, concat_axis=0, tiled=True),
    )
    row_count = local_queries.shape[0]
    blocks_dev = row_count // block_rows
    block_total = blocks_dev * seq_count
    numbers = jnp.arange(block_total, dtype=jnp.int32)
    select = (layout[:, None] == numbers[None, :]).astype(jnp.float32)
    stored = jnp.einsum("jc,hce,ke->hjk", select, block_mask.astype(jnp.float32), select)
    block_ids = seq_index * blocks_dev + jnp.arange(blocks_dev, dtype=jnp.int32)
    pick_rows = (block_ids[:, None] == numbers[None, :]).astype(jnp.float32)
    mask_rows = jnp.einsum("bj,hjk->hbk", pick_rows, stored)
    token_mask = jnp.repeat(mask_rows, block_rows, axis=2) > 0.5
    query_tiles = local_queries.reshape(blocks_dev, block_rows, heads_here, head_width)
    key_piece, value_piece = in_one_piece((local_keys, local_values), "seq", 0, 1)
    length = key_piece.shape[0]
    key_split = key_piece.reshape(length, heads_here, head_width)
    value_split = value_piece.reshape(length, heads_here, head_width)
    maxima = jnp.full((heads_here, blocks_dev, block_rows), -jnp.inf, jnp.float32)
    totals = jnp.zeros((heads_here, blocks_dev, block_rows), jnp.float32)
    accums = jnp.zeros((heads_here, blocks_dev, block_rows, head_width), jnp.float32)
    new_maxima = []
    new_totals = []
    new_accums = []
    for which_head in range(heads_here):
        key_head = key_split[:, which_head, :]
        value_head = value_split[:, which_head, :]
        head_maxima = []
        head_totals = []
        head_accums = []
        for which_block in range(blocks_dev):
            allowed = token_mask[which_head, which_block]
            query_tile = query_tiles[which_block, :, which_head, :]

            def update(
                operands,
                allowed=allowed,
                query_tile=query_tile,
                key_head=key_head,
                value_head=value_head,
            ):
                old_max, old_total, old_accum = operands
                scores = (
                    lax.dot_general(
                        query_tile,
                        key_head,
                        (((1,), (1,)), ((), ())),
                        preferred_element_type=jnp.float32,
                    )
                    * scale
                )
                scores = jnp.where(allowed[None, :], scores, -jnp.inf)
                new_max = jnp.max(scores, axis=1)
                factor = jnp.exp(old_max - new_max)
                probs = jnp.exp(scores - new_max[:, None])
                total = old_total * factor + jnp.sum(probs, axis=1)
                weights = probs.astype(jnp.bfloat16)
                accum = old_accum * factor[:, None] + jnp.dot(
                    weights, value_head, preferred_element_type=jnp.float32
                )
                return (new_max, total, accum)

            def keep(operands):
                return operands

            result = lax.cond(
                jnp.any(allowed),
                update,
                keep,
                (
                    maxima[which_head, which_block],
                    totals[which_head, which_block],
                    accums[which_head, which_block],
                ),
            )
            head_maxima.append(result[0])
            head_totals.append(result[1])
            head_accums.append(result[2])
        new_maxima.append(jnp.stack(head_maxima))
        new_totals.append(jnp.stack(head_totals))
        new_accums.append(jnp.stack(head_accums))
    running = (jnp.stack(new_maxima), jnp.stack(new_totals), jnp.stack(new_accums))
    maxima, totals, accums = running
    outputs = (accums / totals[..., None]).astype(jnp.bfloat16)
    outputs = jnp.transpose(outputs, (1, 2, 0, 3)).reshape(row_count, part_width)
    return lax.all_to_all(outputs, "head", split_axis=0, concat_axis=1, tiled=True)


def solution(mesh):
    placed = (
        P(("seq", "head"), None),
        P(("seq", "head"), None),
        P(("seq", "head"), None),
        P("head", None, None),
        P(),
    )
    return jax.shard_map(
        per_device, mesh=mesh, in_specs=placed, out_specs=P(("seq", "head"), None), check_vma=False
    )
```

profile of v0, /device:TPU:25, one launch (start us, length us, event | category | flops | bytes accessed | tf_op | source)
XLA Modules:
  0.0 562.1 jit_solution(16740743187993856949)
XLA Ops:
  6.5 1.8 copy.165
  8.3 6.6 %all-to-all-start.1 = ((bf16[64,8,384]{2,0,1:T(8,128)(2,1)}), bf16[64,8,384]{2,0,1:T(8,128)(2,1)S(1)}, u32[]{:S(2)}, u32[]{:S(2)}) async-start(bf16[64,8,384]{2,0,1:T(8,128)(2,1)} %bitcast.196), calls=%async_computation.1 | async-start | bytes 786432 | tf_op jit(solution)/shard_map/all_to_all | solution.py:33
  15.9 10.3 %all-to-all-done.1 = bf16[64,8,384]{2,0,1:T(8,128)(2,1)S(1)} async-done(((bf16[64,8,384]{2,0,1:T(8,128)(2,1)}), bf16[64,8,384]{2,0,1:T(8,128)(2,1)S(1)}, u32[]{:S(2)}, u32[]{:S(2)}) %all-to-all-start.1) | async-done | bytes 393248 | tf_op jit(solution)/shard_map/all_to_all | solution.py:33
  26.2 15.2 %all_to_all.73 = bf16[64,8,384]{2,0,1:T(8,128)(2,1)S(1)} all-to-all(bf16[64,8,384]{2,0,1:T(8,128)(2,1)S(1)} %bitcast.201), channel_id=1, replica_groups=mesh['seq'=32,'head'=8] {'head'}, dimensions={1} | all-to-all | bytes 786432 | tf_op jit(solution)/shard_map/all_to_all | solution.py:34
  42.5 1.8 copy.166
  44.3 4.2 all-to-all-start
  50.9 1.9 slice_reduce_fusion.11
  60.3 319.6 %all-gather.2.cloned.1.call-done = bf16[16384,768]{1,0:T(8,128)(2,1)} async-done(((bf16[512,768]{1,0:T(8,128)(2,1)}), bf16[16384,768]{1,0:T(8,128)(2,1)}) %all-gather.2.cloned.1.call-update) | async-done | bytes 25165840 | tf_op jit(solution)/shard_map/all_gather | solution.py:14
  379.9 17.2 %fusion.170 = (bf16[16384,384]{1,0:T(8,128)(2,1)}, bf16[16384,384]{1,0:T(8,128)(2,1)}) fusion(bf16[16384,768]{1,0:T(8,128)(2,1)} %all-gather.2.cloned.1.call-done), kind=kLoop, calls=%fused_computation.200 | loop fusion | bytes 50331648 | tf_op jit(solution)/shard_map/slice | solution.py:16
  397.1 16.7 %copy.93 = bf16[16384,384]{0,1:T(8,128)(2,1)} copy(bf16[16384,384]{1,0:T(8,128)(2,1)} %get-tuple-element.450) | data formatting | bytes 25165824 | tf_op jit(solution)/shard_map/slice | solution.py:16
  413.8 16.6 %copy.94 = bf16[16384,384]{0,1:T(8,128)(2,1)} copy(bf16[16384,384]{1,0:T(8,128)(2,1)} %get-tuple-element.449) | data formatting | bytes 25165824 | tf_op jit(solution)/shard_map/slice | solution.py:16
  430.5 17.2 %slice_bitcast_fusion.28 = (bf16[16384,128]{0,1:T(8,128)(2,1)}, bf16[16384,128]{0,1:T(8,128)(2,1)}, bf16[16384,128]{0,1:T(8,128)(2,1)}, bf16[16384,128]{0,1:T(8,...) fusion(bf16[16384,3,128]{0,2,1:T(8,128)(2,1)} %bitcast.199, bf16[16384,3,128]{0,2,1:T(8,128)(2,1)} %bitcast.198), kind=kLoop, calls=%fused_computation.148 | loop fusion | bytes 50331648 | tf_op jit(solution)/shard_map/squeeze | solution.py:59
  447.7 7.3 %conditional.12 = (f32[1,128]{1,0:T(1,128)S(1)}, f32[1,128,128]{2,1,0:T(8,128)S(1)}) conditional(s32[]{:T(128)} %convert_element_type.81, () %tuple.149, (pred[1,1,16384]{2,1,0:T(4,128)(4,1)S(1)}, bf16[4,128,3,128]{3,2,1,0:T(4,128)(2,1)S(1)}, bf16[16384,128]{0,1:T(8,128)(2,1)}, bf16[16384,128]{0,1:T(8,128)(2,1)}) %tuple.150), branch_computations={%region_1.0_spmd, %region_2.5_spmd} | conditional | flops 1088438400 | bytes 51270188 | solution.py:98
  448.0 3.9 fusion.158
  451.9 1.6 fusion.2
  455.0 7.6 %conditional.13 = (f32[1,128]{1,0:T(1,128)S(1)}, f32[1,128,128]{2,1,0:T(8,128)S(1)}) conditional(s32[]{:T(128)} %convert_element_type.82, () %tuple.151, (pred[1,1,16384]{2,1,0:T(4,128)(4,1)S(1)}, bf16[4,128,3,128]{3,2,1,0:T(4,128)(2,1)S(1)}, bf16[16384,128]{0,1:T(8,128)(2,1)}, bf16[16384,128]{0,1:T(8,128)(2,1)}) %tuple.152), branch_computations={%region_6.7_spmd, %region_7.10_spmd} | conditional | flops 1088438400 | bytes 51270188 | solution.py:98
  455.5 3.9 fusion.159
  459.5 1.6 fusion.14
  462.6 7.3 %conditional.14 = (f32[1,128]{1,0:T(1,128)S(1)}, f32[1,128,128]{2,1,0:T(8,128)S(1)}) conditional(s32[]{:T(128)} %convert_element_type.83, () %tuple.153, (pred[1,1,16384]{2,1,0:T(4,128)(4,1)S(1)}, bf16[4,128,3,128]{3,2,1,0:T(4,128)(2,1)S(1)}, bf16[16384,128]{0,1:T(8,128)(2,1)}, bf16[16384,128]{0,1:T(8,128)(2,1)}) %tuple.154), branch_computations={%region_11.12_spmd, %region_12.15_spmd} | conditional | flops 1088438400 | bytes 51270188 | solution.py:98
  462.9 3.9 fusion.160
  466.8 1.6 fusion.26
  469.9 7.7 %conditional.15 = (f32[1,128]{1,0:T(1,128)S(1)}, f32[1,128,128]{2,1,0:T(8,128)S(1)}) conditional(s32[]{:T(128)} %convert_element_type.84, () %tuple.155, (pred[1,1,16384]{2,1,0:T(4,128)(4,1)S(1)}, bf16[4,128,3,128]{3,2,1,0:T(4,128)(2,1)S(1)}, bf16[16384,128]{0,1:T(8,128)(2,1)}, bf16[16384,128]{0,1:T(8,128)(2,1)}) %tuple.156), branch_computations={%region_16.17_spmd, %region_17.20_spmd} | conditional | flops 1088438400 | bytes 51270188 | solution.py:98
  470.6 3.9 fusion.161
  474.6 1.6 fusion.38
  477.7 7.3 %conditional.16 = (f32[1,128]{1,0:T(1,128)S(1)}, f32[1,128,128]{2,1,0:T(8,128)S(1)}) conditional(s32[]{:T(128)} %convert_element_type.85, () %tuple.157, (pred[1,1,16384]{2,1,0:T(4,128)(4,1)S(1)}, bf16[4,128,3,128]{3,2,1,0:T(4,128)(2,1)S(1)}, bf16[16384,128]{0,1:T(8,128)(2,1)}, bf16[16384,128]{0,1:T(8,128)(2,1)}) %tuple.158), branch_computations={%region_21.22_spmd, %region_22.25_spmd} | conditional | flops 1088438400 | bytes 51270188 | solution.py:98
  478.0 3.9 fusion.162
  481.9 1.6 fusion.50
  485.1 7.5 %conditional.17 = (f32[1,128]{1,0:T(1,128)S(1)}, f32[1,128,128]{2,1,0:T(8,128)S(1)}) conditional(s32[]{:T(128)} %convert_element_type.86, () %tuple.159, (pred[1,1,16384]{2,1,0:T(4,128)(4,1)S(1)}, bf16[4,128,3,128]{3,2,1,0:T(4,128)(2,1)S(1)}, bf16[16384,128]{0,1:T(8,128)(2,1)}, bf16[16384,128]{0,1:T(8,128)(2,1)}) %tuple.160), branch_computations={%region_26.27_spmd, %region_27.30_spmd} | conditional | flops 1088438400 | bytes 51270188 | solution.py:98
  485.5 3.9 fusion.163
  489.4 1.6 fusion.62
  492.6 7.3 %conditional.18 = (f32[1,128]{1,0:T(1,128)S(1)}, f32[1,128,128]{2,1,0:T(8,128)S(1)}) conditional(s32[]{:T(128)} %convert_element_type.87, () %tuple.161, (pred[1,1,16384]{2,1,0:T(4,128)(4,1)S(1)}, bf16[4,128,3,128]{3,2,1,0:T(4,128)(2,1)S(1)}, bf16[16384,128]{0,1:T(8,128)(2,1)}, bf16[16384,128]{0,1:T(8,128)(2,1)}) %tuple.162), branch_computations={%region_31.32_spmd, %region_32.35_spmd} | conditional | flops 1088438400 | bytes 51270188 | solution.py:98
  492.9 3.9 fusion.164
  496.8 1.6 fusion.74
  499.9 7.6 %conditional.19 = (f32[1,128]{1,0:T(1,128)S(1)}, f32[1,128,128]{2,1,0:T(8,128)S(1)}) conditional(s32[]{:T(128)} %convert_element_type.88, () %tuple.163, (pred[1,1,16384]{2,1,0:T(4,128)(4,1)S(1)}, bf16[4,128,3,128]{3,2,1,0:T(4,128)(2,1)S(1)}, bf16[16384,128]{0,1:T(8,128)(2,1)}, bf16[16384,128]{0,1:T(8,128)(2,1)}) %tuple.164), branch_computations={%region_36.37_spmd, %region_37.40_spmd} | conditional | flops 1088438400 | bytes 51270188 | solution.py:98
  500.4 3.9 fusion.165
  504.3 1.6 fusion.86
  507.5 7.3 %conditional.20 = (f32[1,128]{1,0:T(1,128)S(1)}, f32[1,128,128]{2,1,0:T(8,128)S(1)}) conditional(s32[]{:T(128)} %convert_element_type.89, () %tuple.165, (pred[1,1,16384]{2,1,0:T(4,128)(4,1)S(1)}, bf16[4,128,3,128]{3,2,1,0:T(4,128)(2,1)S(1)}, bf16[16384,128]{0,1:T(8,128)(2,1)}, bf16[16384,128]{0,1:T(8,128)(2,1)}) %tuple.166), branch_computations={%region_41.42_spmd, %region_42.45_spmd} | conditional | flops 1088438400 | bytes 51270188 | solution.py:98
  507.8 3.9 fusion.166
  511.7 1.6 fusion.98
  514.8 7.6 %conditional.21 = (f32[1,128]{1,0:T(1,128)S(1)}, f32[1,128,128]{2,1,0:T(8,128)S(1)}) conditional(s32[]{:T(128)} %convert_element_type.90, () %tuple.167, (pred[1,1,16384]{2,1,0:T(4,128)(4,1)S(1)}, bf16[4,128,3,128]{3,2,1,0:T(4,128)(2,1)S(1)}, bf16[16384,128]{0,1:T(8,128)(2,1)}, bf16[16384,128]{0,1:T(8,128)(2,1)}) %tuple.168), branch_computations={%region_46.47_spmd, %region_47.50_spmd} | conditional | flops 1088438400 | bytes 51270188 | solution.py:98
  515.4 3.9 fusion.167
  522.4 7.3 %conditional.22 = (f32[1,128]{1,0:T(1,128)S(1)}, f32[1,128,128]{2,1,0:T(8,128)S(1)}) conditional(s32[]{:T(128)} %convert_element_type.91, () %tuple.169, (pred[1,1,16384]{2,1,0:T(4,128)(4,1)S(1)}, bf16[4,128,3,128]{3,2,1,0:T(4,128)(2,1)S(1)}, bf16[16384,128]{0,1:T(8,128)(2,1)}, bf16[16384,128]{0,1:T(8,128)(2,1)}) %tuple.170), branch_computations={%region_51.52_spmd, %region_52.55_spmd} | conditional | flops 1088438400 | bytes 51270188 | solution.py:98
  522.7 3.9 fusion.168
  526.7 1.6 fusion.122
  529.8 7.6 %conditional.23 = (f32[1,128]{1,0:T(1,128)S(1)}, f32[1,128,128]{2,1,0:T(8,128)S(1)}) conditional(s32[]{:T(128)} %convert_element_type.92, () %tuple.171, (pred[1,1,16384]{2,1,0:T(4,128)(4,1)S(1)}, bf16[4,128,3,128]{3,2,1,0:T(4,128)(2,1)S(1)}, bf16[16384,128]{0,1:T(8,128)(2,1)}, bf16[16384,128]{0,1:T(8,128)(2,1)}) %tuple.172), branch_computations={%region_56.57_spmd, %region_57.60_spmd} | conditional | flops 1088438400 | bytes 51270188 | solution.py:98
  530.4 3.9 fusion.169
  534.3 1.6 fusion.134
  538.6 15.5 %all_to_all.74 = bf16[8,64,384]{2,1,0:T(8,128)(2,1)S(1)} all-to-all(bf16[8,64,384]{2,1,0:T(8,128)(2,1)S(1)} %all_to_all.65), channel_id=1, replica_groups=mesh['seq'=32,'head'=8] {'head'}, dimensions={0} | all-to-all | bytes 786432 | tf_op jit(solution)/shard_map/all_to_all | solution.py:118
  (96 shorter events, 29.7 us)
Async XLA Ops:
  8.3 17.9 %all-to-all-start.1 = ((bf16[64,8,384]{2,0,1:T(8,128)(2,1)}), bf16[64,8,384]{2,0,1:T(8,128)(2,1)S(1)}, u32[]{:S(2)}, u32[]{:S(2)}) async-start(bf16[64,8,384]{2,0,1:T(8,128)(2,1)} %bitcast.196), calls=%async_computation.1 | async-start | bytes 786432 | tf_op jit(solution)/shard_map/all_to_all | solution.py:33
  14.9 365.0 %all-gather.2.cloned.1.call-start = ((), (), s32[]{:S(2)}) async-start(), calls=%async_computation.4 | async-start | bytes 25952256 | tf_op jit(solution)/shard_map/all_gather | solution.py:14
  44.3 16.0 %all-to-all-start = ((bf16[64,8,384]{2,0,1:T(8,128)(2,1)}), bf16[64,8,384]{2,0,1:T(8,128)(2,1)S(1)}, u32[]{:S(2)}, u32[]{:S(2)}) async-start(bf16[64,8,384]{2,0,1:T(8,128)(2,1)} %bitcast.197), calls=%async_computation | async-start | bytes 786432 | tf_op jit(solution)/shard_map/all_to_all | solution.py:32
  448.0 5.5 copy-start.8
  455.5 5.5 copy-start.9
  462.9 5.5 copy-start.10
  470.6 5.5 copy-start.11
  478.0 5.5 copy-start.4
  485.5 5.5 copy-start.5
  492.9 5.5 copy-start.6
  500.4 5.5 copy-start.7
  507.8 5.5 copy-start
  515.4 5.5 copy-start.1
  522.7 5.5 copy-start.2
  530.4 5.5 copy-start.3
Sparse Core Ops, SparseCore 0:
  42.6 337.2 all-gather.1
where the time goes:
time: 572 us; the launch traced here: 562 us
  waiting for transfers between devices  330 us (58%)
  local copies, waits for them, and re-layouts  75.8 us (13%)
  matrix products  66.9 us (12%)
  blocking collectives  30.7 us (5%)
  other arithmetic  24.4 us (4%)
  between operations  21.5 us (4%)
  starting transfers between devices  10.8 us (2%)
    all_gather x1, waiting for transfers between devices, in_one_piece(): filled, at, outs = (lax.all_gather(both, axis, axis=dim, tiled=True), 0, [])  320 us
    slice x3, local copies, waits for them, and re-layouts, in_one_piece(): outs.append(lax.slice_in_dim(filled, at, at + a.shape[along], axis=along))  50.6 us
    dot_general x12, matrix products, update(): lax.dot_general(query_tile, key_head, (((1,), (1,)), ((), ())), preferred...  46.9 us
    reduce_sum x12, other arithmetic, update(): total = old_total * factor + jnp.sum(probs, axis=1)  18.9 us
    dot_general x12, matrix products, update(): jnp.dot(weights, value_head, preferred_element_type=jnp.float32)  18.5 us
    squeeze x1, local copies, waits for them, and re-layouts, per_device(): value_head = value_split[:, which_head, :]  17.2 us
    all_to_all x1, blocking collectives, per_device(): lax.all_to_all(outputs, 'head', split_axis=0, concat_axis=1, tiled=True)  15.5 us
    all_to_all x1, blocking collectives, per_device(): lax.all_to_all(value_vectors, 'head', split_axis=1, concat_axis=0, tiled=...  15.2 us
  transfers between devices with their start and end apart: 3, of which 2 were waited for; matrix products, arithmetic and copies ran while one was open for 1% of the time, Pallas kernels for 0%

commit v1 on v0

v1 whole, which is shorter than its diff:
```python
import math

import jax
import jax.numpy as jnp
from jax import lax
from jax.experimental import pallas as pl
from jax.experimental.pallas import tpu as pltpu
from jax.sharding import Mesh, PartitionSpec as P

HEAD = 128
BLOCK = 128
HALF = 64
NX, NY, NZ = 4, 4, 8
HEADS_HERE = 3
SLAB = HEADS_HERE * HEAD
ITEMS = NX * (NZ // 2)
KBLOCKS = NY * NZ
UNROLL = 4
NEG = -1e30
BIG = 1e30
COEF = math.log2(math.e) / math.sqrt(HEAD)
MESH = pl.DeviceIdType.MESH
ORDER = (1, 7, 2, 6, 3, 5, 4)


def place():
    x, y = lax.axis_index("x"), lax.axis_index("y")
    z = lax.axis_index("zh") * 4 + lax.axis_index("zl")
    return x, y, z, lax.axis_index("c")


def device(x, y, z, c):
    return (x, y, z // 4, z % 4, c)


def group(z):
    return (z % 4) * 2 + z // 4


def gather_kernel(q_in, k_in, v_in, mask_in, kv, q, mask,
                  zs_send, z_recv, q_send, q_recv, y_send, y_recv, f_send, f_recv,
                  s_send, s_recv, x_send, x_recv, xf_send, xf_recv, own, mask_sem):
    x, y, z, c = place()
    other = 1 - c
    parity = z % 2
    yn, yp = (y + 1) % NY, (y + NY - 1) % NY
    xn, xp = (x + 1) % NX, (x + NX - 1) % NX
    y2, x2 = (y + 2) % NY, (x + 2) % NX

    def remote(src, dst, send, recv, dev):
        return pltpu.make_async_remote_copy(
            src_ref=src, dst_ref=dst, send_sem=send, recv_sem=recv,
            device_id=dev, device_id_type=MESH)

    barrier = pltpu.get_barrier_semaphore()
    peers = [device(x, y, (z + d) % NZ, cc) for d in range(1, NZ) for cc in range(2)]
    peers += [device(x, y, z, other), device(x, yn, z, c), device(x, yp, z, c),
              device(xn, y, z, c), device(xp, y, z, c)]
    for peer in peers:
        pl.semaphore_signal(barrier, inc=1, device_id=peer, device_id_type=MESH)
    pl.semaphore_wait(barrier, len(peers))

    def columns(zd):
        return pl.ds(pl.multiple_of(group(zd) * SLAB, SLAB), SLAB)

    def k_cols():
        return pl.ds(0, SLAB)

    def v_cols():
        return pl.ds(SLAB, SLAB)

    mine = columns(z)
    own_k = pltpu.make_async_copy(k_in.at[:, mine], kv.at[y, z, c, :, k_cols()], own.at[0])
    own_v = pltpu.make_async_copy(v_in.at[:, mine], kv.at[y, z, c, :, v_cols()], own.at[1])
    own_k.start()
    own_v.start()

    sends = []
    half = z // 2

    def start(copy):
        copy.start()
        sends.append(copy)

    def own_q_copies():
        return (
            pltpu.make_async_copy(q_in.at[:, mine], q.at[x, half, c], own.at[2]),
            remote(q_in.at[:, mine], q.at[x, half, c], q_send.at[0], q_recv.at[half, c],
                   device(x, y, z, other)),
        )

    for d in ORDER:
        zd = (z + d) % NZ
        cols = columns(zd)
        start(remote(k_in.at[:, cols], kv.at[y, z, c, :, k_cols()],
                     zs_send.at[0, d], z_recv.at[0, d], device(x, y, zd, c)))
        start(remote(v_in.at[:, cols], kv.at[y, z, c, :, v_cols()],
                     zs_send.at[1, d], z_recv.at[1, d], device(x, y, zd, c)))
        start(remote(q_in.at[:, cols], q.at[x, half, c],
                     q_send.at[d], q_recv.at[half, c], device(x, y, zd, parity)))

    @pl.when(c == parity)
    def _():
        own_q_copies()[0].start()

    @pl.when(c != parity)
    def _():
        own_q_copies()[1].start()

    swap = remote(mask_in, mask, mask_sem.at[0], mask_sem.at[1], device(x, y, z, other))
    swap.start()

    def waiter(dst, recv):
        return remote(dst, dst, recv, recv, device(x, y, z, other))

    def spread(d):
        zs = (z - d + NZ) % NZ
        piece = kv.at[y, zs, c]
        if d == 0:
            own_k.wait()
            own_v.wait()
        else:
            waiter(kv.at[y, zs, c, :, k_cols()], z_recv.at[0, d]).wait_recv()
            waiter(kv.at[y, zs, c, :, v_cols()], z_recv.at[1, d]).wait_recv()
        start(remote(piece, piece, y_send.at[0, d], y_recv.at[0, d], device(x, yn, z, c)))
        start(remote(piece, piece, y_send.at[1, d], y_recv.at[1, d], device(x, yp, z, c)))
        start(remote(piece, piece, s_send.at[0, d], s_recv.at[0, d], device(x, y, z, other)))

    def relay(d):
        zs = (z - d + NZ) % NZ
        for way, (row, ahead) in enumerate(((yp, yn), (yn, yp))):
            piece = kv.at[row, zs, c]
            waiter(piece, y_recv.at[way, d]).wait_recv()
            if d % 2 == way:
                start(remote(piece, piece, f_send.at[d], f_recv.at[d], device(x, ahead, z, c)))
            start(remote(piece, piece, s_send.at[1 + way, d], s_recv.at[1 + way, d],
                         device(x, y, z, other)))

    def spread_q(i):
        for cc in range(2):
            piece = q.at[x, i, cc]
            local = (c == parity) & (i == half) & (c == cc)

            @pl.when(local)
            def _():
                own_q_copies()[0].wait()

            @pl.when(jnp.logical_not(local))
            def _():
                waiter(piece, q_recv.at[i, cc]).wait_recv()

        piece = q.at[x, i]
        start(remote(piece, piece, x_send.at[0, i], x_recv.at[0, i], device(xn, y, z, c)))
        start(remote(piece, piece, x_send.at[1, i], x_recv.at[1, i], device(xp, y, z, c)))

    def relay_q(i):
        for way, (row, ahead) in enumerate(((xp, xn), (xn, xp))):
            piece = q.at[row, i]
            waiter(piece, x_recv.at[way, i]).wait_recv()
            if i % 2 == way:
                start(remote(piece, piece, xf_send.at[i], xf_recv.at[i], device(ahead, y, z, c)))

    seq = (0,) + ORDER
    for step in range(len(seq) + 2):
        if step < len(seq):
            spread(seq[step])
        if step >= 2:
            relay(seq[step - 2])
    for i in range(4):
        spread_q(i)
    for d in seq:
        zs = (z - d + NZ) % NZ
        piece = kv.at[y2, zs, c]
        waiter(piece, f_recv.at[d]).wait_recv()
        start(remote(piece, piece, s_send.at[3, d], s_recv.at[3, d], device(x, y, z, other)))
    for i in range(4):
        relay_q(i)
    for i in range(4):
        waiter(q.at[x2, i], xf_recv.at[i]).wait_recv()
    for d in seq:
        zs = (z - d + NZ) % NZ
        for slot, row in enumerate((y, yp, yn, y2)):
            waiter(kv.at[row, zs, other], s_recv.at[slot, d]).wait_recv()
    swap.wait()

    @pl.when(c != parity)
    def _():
        own_q_copies()[1].wait_send()

    for copy in sends:
        copy.wait_send()


def gather(queries, keys, values, block_mask):
    any_space = pl.BlockSpec(memory_space=pl.ANY)
    vmem = pl.BlockSpec(memory_space=pltpu.VMEM)
    dma = pltpu.SemaphoreType.DMA
    return pl.pallas_call(
        gather_kernel,
        out_shape=(
            jax.ShapeDtypeStruct((NY, NZ, 2, HALF, 2 * SLAB), jnp.bfloat16),
            jax.ShapeDtypeStruct((NX, NZ // 2, 2, HALF, SLAB), jnp.bfloat16),
            jax.ShapeDtypeStruct(block_mask.shape, block_mask.dtype),
        ),
        in_specs=[vmem, vmem, vmem, any_space],
        out_specs=(any_space, any_space, any_space),
        scratch_shapes=[
            dma((2, NZ)), dma((2, NZ)), dma((NZ,)), dma((4, 2)),
            dma((2, NZ)), dma((2, NZ)), dma((NZ,)), dma((NZ,)),
            dma((4, NZ)), dma((4, NZ)),
            dma((2, 4)), dma((2, 4)), dma((4,)), dma((4,)), dma((3,)), dma((2,)),
        ],
        compiler_params=pltpu.CompilerParams(collective_id=0, has_side_effects=True),
        name="gather",
    )(queries, keys, values, block_mask)


def attend_kernel(blocks, counts, kv_ref, q_ref, o_ref, stat_ref, vt, s0, s1, acc, m_ref, l_ref):
    total_items = HEADS_HERE * ITEMS

    for head in range(HEADS_HERE):
        @pl.loop(0, KBLOCKS)
        def _(b, head=head):
            vt[head, b] = kv_ref[b, :, SLAB + head * HEAD:SLAB + (head + 1) * HEAD].T

    def steps_of(item):
        return jnp.maximum((counts[item] + UNROLL - 1) // UNROLL, 1)

    steps = lax.fori_loop(0, total_items, lambda i, n: n + steps_of(i), 0)

    def ids(item, at):
        return [blocks[item * KBLOCKS + at + u] for u in range(UNROLL)]

    def score(item, at, out):
        head = item // ITEMS
        cols = pl.ds(pl.multiple_of(head * HEAD, HEAD), HEAD)
        rows = [kv_ref[b, :, cols] for b in ids(item, at)]
        out[...] = lax.dot_general(jnp.concatenate(rows, axis=0), q_ref[item % ITEMS, :, cols],
                                   (((1,), (1,)), ((), ())), preferred_element_type=jnp.float32)

    def absorb(item, at, src):
        head = item // ITEMS
        first = at == 0
        count = counts[item]
        m_old = jnp.where(first, NEG, m_ref[...])
        t = [src[u * BLOCK:(u + 1) * BLOCK] * COEF for u in range(UNROLL)]
        valid = [at + u < count for u in range(UNROLL)]
        m_new = m_old
        for u in range(UNROLL):
            m_new = jnp.maximum(m_new, jnp.where(valid[u], jnp.max(t[u], axis=0, keepdims=True), NEG))
        alpha = jnp.where(first, 0.0, jnp.exp2(m_old - m_new))
        summed = l_ref[...] * alpha
        weights = []
        for u in range(UNROLL):
            p = jnp.exp2(t[u] - jnp.where(valid[u], m_new, BIG))
            summed = summed + jnp.sum(p, axis=0, keepdims=True)
            weights.append(p.astype(jnp.bfloat16))
        cols = [vt[head, b] for b in ids(item, at)]
        value = acc[...] * alpha + jnp.dot(
            jnp.concatenate(cols, axis=1), jnp.concatenate(weights, axis=0),
            preferred_element_type=jnp.float32)
        acc[...] = value
        m_ref[...] = m_new
        l_ref[...] = summed

        @pl.when(at + UNROLL >= count)
        def _():
            where = item % ITEMS
            o_ref[where, pl.ds(pl.multiple_of(head * HEAD, HEAD), HEAD), :] = value.astype(jnp.bfloat16)
            stat_ref[where, pl.ds(2 * head, 1), :] = m_new
            stat_ref[where, pl.ds(2 * head + 1, 1), :] = summed

    def advance(item, at):
        done = at + UNROLL >= counts[item]
        item = jnp.minimum(jnp.where(done, item + 1, item), total_items - 1)
        return item, jnp.where(done, 0, at + UNROLL)

    acc[...] = jnp.zeros_like(acc)
    m_ref[...] = jnp.full_like(m_ref, NEG)
    l_ref[...] = jnp.zeros_like(l_ref)
    score(jnp.int32(0), jnp.int32(0), s0)

    def pair(_, state):
        item0, at0 = state
        item1, at1 = advance(item0, at0)
        score(item1, at1, s1)
        absorb(item0, at0, s0)
        item2, at2 = advance(item1, at1)
        score(item2, at2, s0)
        absorb(item1, at1, s1)
        return item2, at2

    lax.fori_loop(0, (steps + 1) // 2, pair, (jnp.int32(0), jnp.int32(0)))


def attend(blocks, counts, kv, queries):
    vmem = pl.BlockSpec(memory_space=pltpu.VMEM)
    smem = pl.BlockSpec(memory_space=pltpu.SMEM)
    return pl.pallas_call(
        attend_kernel,
        out_shape=(
            jax.ShapeDtypeStruct((ITEMS, SLAB, BLOCK), jnp.bfloat16),
            jax.ShapeDtypeStruct((ITEMS, 8, BLOCK), jnp.float32),
        ),
        in_specs=[smem, smem, vmem, vmem],
        out_specs=(vmem, vmem),
        scratch_shapes=[
            pltpu.VMEM((HEADS_HERE, KBLOCKS, HEAD, BLOCK), jnp.bfloat16),
            pltpu.VMEM((UNROLL * BLOCK, BLOCK), jnp.float32),
            pltpu.VMEM((UNROLL * BLOCK, BLOCK), jnp.float32),
            pltpu.VMEM((HEAD, BLOCK), jnp.float32),
            pltpu.VMEM((1, BLOCK), jnp.float32),
            pltpu.VMEM((1, BLOCK), jnp.float32),
        ],
        name="attend",
    )(blocks, counts, kv, queries)


def merge_kernel(o_in, stat_in, out, o_all, stat_all, result, x_send, x_recv, st_send, st_recv,
                 z_send, z_recv, own):
    x, y, z, c = place()
    other = 1 - c

    def remote(src, dst, send, recv, dev):
        return pltpu.make_async_remote_copy(
            src_ref=src, dst_ref=dst, send_sem=send, recv_sem=recv,
            device_id=dev, device_id_type=MESH)

    barrier = pltpu.get_barrier_semaphore()
    peers = [device(x, y, (z + d) % NZ, cc) for d in range(1, NZ) for cc in range(2)]
    peers += [device(x, y, z, other)] + [device((x + d) % NX, y, z, c) for d in range(1, NX)]
    for peer in peers:
        pl.semaphore_signal(barrier, inc=1, device_id=peer, device_id_type=MESH)
    pl.semaphore_wait(barrier, len(peers))

    sends = []
    for d in (2, 1, 3):
        xd = (x + d) % NX
        dev = device(xd, y, z, c)
        sends.append(remote(stat_in.at[xd], stat_all.at[x], st_send.at[d], st_recv.at[d], dev))
        sends[-1].start()
        for i in range(4):
            sends.append(remote(o_in.at[xd, i], o_all.at[x, i], x_send.at[d, i], x_recv.at[d, i], dev))
            sends[-1].start()
    keep_o = pltpu.make_async_copy(o_in.at[x], o_all.at[x], own.at[0])
    keep_s = pltpu.make_async_copy(stat_in.at[x], stat_all.at[x], own.at[1])
    keep_o.start()
    keep_s.start()

    def waiter(dst, recv):
        return remote(dst, dst, recv, recv, device(x, y, z, other))

    keep_s.wait()
    keep_o.wait()
    for d in (1, 3, 2):
        waiter(stat_all.at[(x - d + NX) % NX], st_recv.at[d]).wait_recv()

    def columns(zd):
        return pl.ds(pl.multiple_of(group(zd) * SLAB, SLAB), SLAB)

    def local_of(i, cc):
        src = result.at[i, pl.ds(cc * HALF, HALF)]
        return pltpu.make_async_copy(src, out.at[:, columns(z)], own.at[2])

    def remote_of(i, cc):
        src = result.at[i, pl.ds(cc * HALF, HALF)]
        return remote(src, out.at[:, columns(z)], z_send.at[i, cc], z_recv.at[z],
                      device(x, y, 2 * i + c, cc))

    def is_local(i, cc):
        return (2 * i + c == z) & (c == cc)

    def ship(i):
        for cc in range(2):
            @pl.when(is_local(i, cc))
            def _():
                local_of(i, cc).start()

            @pl.when(jnp.logical_not(is_local(i, cc)))
            def _():
                remote_of(i, cc).start()

    for i in range(4):
        for d in (1, 3, 2):
            waiter(o_all.at[(x - d + NX) % NX, i], x_recv.at[d, i]).wait_recv()
        for head in range(HEADS_HERE):
            m = [stat_all[s, i, 2 * head:2 * head + 1, :] for s in range(NX)]
            top = jnp.maximum(jnp.maximum(m[0], m[1]), jnp.maximum(m[2], m[3]))
            w = [jnp.exp2(v - top) for v in m]
            total = sum(w[s] * stat_all[s, i, 2 * head + 1:2 * head + 2, :] for s in range(NX))
            rows = slice(head * HEAD, (head + 1) * HEAD)
            value = sum(o_all[s, i, rows, :].astype(jnp.float32) * w[s] for s in range(NX))
            result[i, :, rows] = (value / total).T.astype(jnp.bfloat16)
        if i:
            ship(i - 1)
    ship(3)

    for zs in range(NZ):
        local = (zs == z) & (zs % 2 == c)

        @pl.when(jnp.logical_not(local))
        def _(zs=zs):
            waiter(out.at[:, columns(zs)], z_recv.at[zs]).wait_recv()
    for i in range(4):
        for cc in range(2):
            @pl.when(is_local(i, cc))
            def _():
                local_of(i, cc).wait()

            @pl.when(jnp.logical_not(is_local(i, cc)))
            def _():
                remote_of(i, cc).wait_send()
    for copy in sends:
        copy.wait_send()


def merge(partial, stats):
    any_space = pl.BlockSpec(memory_space=pl.ANY)
    dma = pltpu.SemaphoreType.DMA
    return pl.pallas_call(
        merge_kernel,
        out_shape=jax.ShapeDtypeStruct((HALF, NZ * SLAB), jnp.bfloat16),
        in_specs=[any_space, any_space],
        out_specs=any_space,
        scratch_shapes=[
            pltpu.VMEM((NX, 4, SLAB, BLOCK), jnp.bfloat16),
            pltpu.VMEM((NX, 4, 8, BLOCK), jnp.float32),
            pltpu.VMEM((4, BLOCK, SLAB), jnp.bfloat16),
            dma((NX, 4)), dma((NX, 4)), dma((NX,)), dma((NX,)),
            dma((4, 2)), dma((NZ,)), dma((3,)),
        ],
        compiler_params=pltpu.CompilerParams(collective_id=1, has_side_effects=True),
        name="merge",
    )(partial, stats)


def block_lists(block_mask, swapped, layout):
    x, y, z, c = place()
    mask = jnp.where(c == lax.axis_index("zh"), block_mask, swapped)
    numbers = jnp.arange(KBLOCKS * NX, dtype=jnp.int32)
    item = jnp.arange(ITEMS, dtype=jnp.int32)
    rows = 32 * (item // 4) + 8 * y + 2 * (item % 4) + c
    cols = 32 * x + jnp.arange(KBLOCKS, dtype=jnp.int32)
    select = layout[:, None] == numbers[None, :]

    def picker(stored):
        hit = (stored[:, None] == numbers[None, :]).astype(jnp.bfloat16)
        return jnp.dot(hit, select.astype(jnp.bfloat16), preferred_element_type=jnp.float32).astype(jnp.bfloat16)

    some = jnp.einsum("ic,hcd->hid", picker(rows), mask.astype(jnp.bfloat16),
                      preferred_element_type=jnp.float32).astype(jnp.bfloat16)
    allowed = jnp.einsum("hid,kd->hik", some, picker(cols), preferred_element_type=jnp.float32) > 0.5
    spot = jnp.arange(KBLOCKS, dtype=jnp.int32)
    before = (spot[:, None] < spot[None, :]).astype(jnp.bfloat16)
    rank = jnp.einsum("hik,kj->hij", allowed.astype(jnp.bfloat16), before,
                      preferred_element_type=jnp.float32).astype(jnp.int32)
    hit = allowed[..., None] & (rank[..., None] == spot)
    blocks = jnp.sum(jnp.where(hit, spot[:, None], 0), axis=2)
    counts = jnp.sum(allowed.astype(jnp.int32), axis=2)
    return blocks.reshape(-1), counts.reshape(-1)


def per_device(queries, keys, values, block_mask, layout):
    kv, q, swapped = gather(queries, keys, values, block_mask)
    blocks, counts = block_lists(block_mask, swapped, layout)
    partial, stats = attend(blocks, counts, kv.reshape(KBLOCKS, BLOCK, 2 * SLAB),
                            q.reshape(ITEMS, BLOCK, SLAB))
    return merge(partial.reshape(NX, 4, SLAB, BLOCK), stats.reshape(NX, 4, 8, BLOCK))


def solution(mesh):
    grid = Mesh(mesh.devices.reshape(NX, NY, 2, 4, 2), ("x", "y", "zh", "zl", "c"))
    rows = P(("x", "y", "zh", "zl", "c"), None)
    return jax.shard_map(
        per_device, mesh=grid,
        in_specs=(rows, rows, rows, P(("zl", "c"), None, None), P()),
        out_specs=rows, check_vma=False)
```

time: 572 us -> 159 us (0.28); the launches traced: 562 us -> 159 us
  waiting for transfers between devices: 330 us -> 0 us
  Pallas kernels: 0 us -> 152 us
  local copies, waits for them, and re-layouts: 75.8 us -> 3.12 us
  matrix products: 66.9 us -> 3.08 us
  blocking collectives: 30.7 us -> 0 us
  other arithmetic: 24.4 us -> 0.73 us
  between operations: 21.5 us -> 0.05 us
  starting transfers between devices: 10.8 us -> 0 us
    all_gather x1 -> x0, waiting for transfers between devices: 320 us -> none  [in_one_piece(): filled, at, outs = (lax.all_gather(both, axis, axis=dim, tiled=True), 0, [])]
    pallas_call x0 -> x3, Pallas kernels: none -> 152 us  [the longest x1 60.4 us: attend(): pl.pallas_call(attend_kernel, out_shape=(jax.ShapeDtypeStruct((ITEMS, SLA...]
    dot_general x26 -> x4, matrix products: 66.9 us -> 3.08 us  [the longest x2 1.75 us: picker(): jnp.dot(hit, select.astype(jnp.bfloat16), preferred_element_type=jnp.floa...]
    slice x4 -> x0, local copies, waits for them, and re-layouts: 51 us -> none  [the longest x3 50.6 us: in_one_piece(): outs.append(lax.slice_in_dim(filled, at, at + a.shape[along], axis=along))]
    all_to_all x2 -> x0, blocking collectives: 30.7 us -> none  [the longest x1 15.5 us: per_device(): lax.all_to_all(outputs, 'head', split_axis=0, concat_axis=1, tiled=True)]
    reduce_sum x12 -> x2, other arithmetic: 18.9 us -> 0.71 us  [the longest x1 0.57 us: block_lists(): blocks = jnp.sum(jnp.where(hit, spot[:, None], 0), axis=2)]
    squeeze x1 -> x0, local copies, waits for them, and re-layouts: 17.2 us -> none  [per_device(): value_head = value_split[:, which_head, :]]
    all_to_all x2 -> x0, starting transfers between devices: 10.8 us -> none  [the longest x1 6.57 us: per_device(): lax.all_to_all(key_vectors, 'head', split_axis=1, concat_axis=0, tiled=True)]
  transfers between devices with their start and end apart: 3 -> 0, of which waited for: 2 -> 0; matrix products, arithmetic and copies ran while one was open for 1% -> 0% of each run, Pallas kernels for 0% -> 0%
where the time goes in v1:
time: 159 us
  Pallas kernels  152 us (96%)
  local copies, waits for them, and re-layouts  3.12 us (2%)
  matrix products  3.08 us (2%)
    pallas_call x1, Pallas kernels, attend(): pl.pallas_call(attend_kernel, out_shape=(jax.ShapeDtypeStruct((ITEMS, SLA...  60.4 us
    pallas_call x1, Pallas kernels, gather(): pl.pallas_call(gather_kernel, out_shape=(jax.ShapeDtypeStruct((NY, NZ, 2,...  52.9 us
    pallas_call x1, Pallas kernels, merge(): pl.pallas_call(merge_kernel, out_shape=jax.ShapeDtypeStruct((HALF, NZ * S...  38.6 us

profile of v1, /device:TPU:25, one launch (start us, length us, event | category | flops | bytes accessed | tf_op | source)
XLA Modules:
  0.0 158.9 jit_solution(9897944031560424631)
XLA Ops:
  0.0 0.0 copy-start
  0.0 0.9 fusion.5
  0.9 0.9 fusion.4
  1.8 52.9 %gather.1 = (bf16[4,8,2,64,768]{4,3,2,1,0:T(8,128)(2,1)}, bf16[4,4,2,64,384]{4,3,2,1,0:T(8,128)(2,1)}, s32[3,128,128]{2,1,0:T(8,128)}) custom-call(bf16[64,3072]{1,0:T(8,128)(2,1)} %q_in.1, bf16[64,3072]{1,0:T(8,128)(2,1)} %k_in.1, bf16[64,3072]{1,0:T(8,128)(2,1)} %v_in.1, s32[3,128,128]{2,1,0:T(8,128)} %mask_in.1), custom_call_target="tpu_custom_call" | custom-call | tf_op jit(solution)/shard_map/gather/pallas_call | solution.py:198
  54.7 0.0 copy-done
  54.7 1.2 fusion.6
  55.9 0.1 convert_reduce_fusion
  56.0 0.7 reshape.51.counts
  56.7 0.1 convolution_convert_fusion
  56.9 0.6 select_reduce_fusion
  57.4 0.7 reshape.50.blocks
  58.1 60.4 %attend.1 = (bf16[16,384,128]{2,1,0:T(8,128)(2,1)}, f32[16,8,128]{2,1,0:T(8,128)}) custom-call(s32[1536]{0:T(1024)} %reshape.50.blocks, s32[48]{0:T(128)} %reshape.51.counts, bf16[32,128,768]{2,1,0:T(8,128)(2,1)} %bitcast.20, bf16[16,128,384]{2,1,0:T(8,128)(2,1)} %bitcast.21), custom_call_target="tpu_custom_call" | custom-call | tf_op jit(solution)/shard_map/attend/pallas_call | solution.py:299
  118.5 38.6 %merge.1 = bf16[64,3072]{1,0:T(8,128)(2,1)} custom-call(bf16[4,4,384,128]{3,2,1,0:T(8,128)(2,1)} %bitcast.22, f32[4,4,8,128]{3,2,1,0:T(8,128)} %bitcast.23), custom_call_target="tpu_custom_call" | custom-call | tf_op jit(solution)/shard_map/merge/pallas_call | solution.py:420
  157.1 1.8 %copy.7 = bf16[64,3072]{1,0:T(8,128)(2,1)} copy(bf16[64,3072]{1,0:T(8,128)(2,1)} %merge.1) | data formatting | bytes 786432
  (3 shorter events, 0.0 us)
Async XLA Ops:
  0.0 54.7 %copy-start = (s32[3,128,128]{2,1,0:T(8,128)S(1)}, s32[3,128,128]{2,1,0:T(8,128)}, u32[]{:S(2)}) copy-start(s32[3,128,128]{2,1,0:T(8,128)} %mask_in.1) | copy-start | bytes 589828

commit v2 on v1

--- a/solution.py
+++ b/solution.py
@@ -215,82 +215,98 @@
     )(queries, keys, values, block_mask)
 
 
-def attend_kernel(blocks, counts, kv_ref, q_ref, o_ref, stat_ref, vt, s0, s1, acc, m_ref, l_ref):
+def attend_kernel(blocks, counts, kv_ref, q_ref, o_ref, stat_ref, vt, qt, s0, s1, p0, p1, acc, m_ref, l_ref):
     total_items = HEADS_HERE * ITEMS
 
     for head in range(HEADS_HERE):
         @pl.loop(0, KBLOCKS)
         def _(b, head=head):
-            vt[head, b] = kv_ref[b, :, SLAB + head * HEAD:SLAB + (head + 1) * HEAD].T
+            vt[head * KBLOCKS + b] = kv_ref[b, :, SLAB + head * HEAD:SLAB + (head + 1) * HEAD].T
+
+        @pl.loop(0, ITEMS)
+        def _(i, head=head):
+            qt[head * ITEMS + i] = q_ref[i, :, head * HEAD:(head + 1) * HEAD].T
 
     def steps_of(item):
-        return jnp.maximum((counts[item] + UNROLL - 1) // UNROLL, 1)
+        return jnp.maximum((counts[item] + UNROLL - 1) >> 2, 1)
 
     steps = lax.fori_loop(0, total_items, lambda i, n: n + steps_of(i), 0)
 
-    def ids(item, at):
-        return [blocks[item * KBLOCKS + at + u] for u in range(UNROLL)]
+    def home(item):
+        spare = item == total_items
+        return jnp.where(spare, ITEMS, item & (ITEMS - 1)), jnp.where(spare, 0, item >> 4)
 
     def score(item, at, out):
-        head = item // ITEMS
-        cols = pl.ds(pl.multiple_of(head * HEAD, HEAD), HEAD)
-        rows = [kv_ref[b, :, cols] for b in ids(item, at)]
-        out[...] = lax.dot_general(jnp.concatenate(rows, axis=0), q_ref[item % ITEMS, :, cols],
-                                   (((1,), (1,)), ((), ())), preferred_element_type=jnp.float32)
-
-    def absorb(item, at, src):
-        head = item // ITEMS
+        base = item * KBLOCKS + at
+        left = counts[item] - at
+        cols = pl.ds(pl.multiple_of(home(item)[1] * HEAD, HEAD), HEAD)
+        rows = [kv_ref[blocks[base + u], :, cols] for u in range(UNROLL)]
+        t = jnp.dot(jnp.concatenate(rows, axis=0), qt[item], preferred_element_type=jnp.float32) * COEF
+        out[...] = t
+        peak = jnp.full((1, BLOCK), NEG, jnp.float32)
+        for u in range(UNROLL):
+            part = jnp.max(t[u * BLOCK:(u + 1) * BLOCK], axis=0, keepdims=True)
+            peak = jnp.maximum(peak, jnp.where(u < left, part, NEG))
+        return peak
+
+    def soften(chunk, peak, src, out):
+        item, at = chunk
         first = at == 0
-        count = counts[item]
+        left = counts[item] - at
         m_old = jnp.where(first, NEG, m_ref[...])
-        t = [src[u * BLOCK:(u + 1) * BLOCK] * COEF for u in range(UNROLL)]
-        valid = [at + u < count for u in range(UNROLL)]
-        m_new = m_old
-        for u in range(UNROLL):
-            m_new = jnp.maximum(m_new, jnp.where(valid[u], jnp.max(t[u], axis=0, keepdims=True), NEG))
+        m_new = jnp.maximum(m_old, peak)
         alpha = jnp.where(first, 0.0, jnp.exp2(m_old - m_new))
         summed = l_ref[...] * alpha
-        weights = []
         for u in range(UNROLL):
-            p = jnp.exp2(t[u] - jnp.where(valid[u], m_new, BIG))
+            rows = slice(u * BLOCK, (u + 1) * BLOCK)
+            p = jnp.exp2(src[rows] - jnp.where(u < left, m_new, BIG))
             summed = summed + jnp.sum(p, axis=0, keepdims=True)
-            weights.append(p.astype(jnp.bfloat16))
-        cols = [vt[head, b] for b in ids(item, at)]
-        value = acc[...] * alpha + jnp.dot(
-            jnp.concatenate(cols, axis=1), jnp.concatenate(weights, axis=0),
-            preferred_element_type=jnp.float32)
-        acc[...] = value
+            out[rows] = p.astype(jnp.bfloat16)
         m_ref[...] = m_new
         l_ref[...] = summed
 
-        @pl.when(at + UNROLL >= count)
-        def _():
-            where = item % ITEMS
-            o_ref[where, pl.ds(pl.multiple_of(head * HEAD, HEAD), HEAD), :] = value.astype(jnp.bfloat16)
-            stat_ref[where, pl.ds(2 * head, 1), :] = m_new
-            stat_ref[where, pl.ds(2 * head + 1, 1), :] = summed
-
-    def advance(item, at):
+        where, head = home(item)
+        stat_ref[where, pl.ds(2 * head, 1), :] = m_new
+        stat_ref[where, pl.ds(2 * head + 1, 1), :] = summed
+        return alpha
+
+    def gather_values(chunk, alpha, src):
+        item, at = chunk
+        base = item * KBLOCKS + at
+        where, head = home(item)
+        cols = [vt[head * KBLOCKS + blocks[base + u]] for u in range(UNROLL)]
+        value = acc[...] * alpha + jnp.dot(jnp.concatenate(cols, axis=1), src[...],
+                                           preferred_element_type=jnp.float32)
+        acc[...] = value
+        o_ref[where, pl.ds(pl.multiple_of(head * HEAD, HEAD), HEAD), :] = value.astype(jnp.bfloat16)
+
+    def advance(chunk):
+        item, at = chunk
         done = at + UNROLL >= counts[item]
-        item = jnp.minimum(jnp.where(done, item + 1, item), total_items - 1)
-        return item, jnp.where(done, 0, at + UNROLL)
+        return jnp.minimum(jnp.where(done, item + 1, item), total_items), jnp.where(done, 0, at + UNROLL)
 
     acc[...] = jnp.zeros_like(acc)
     m_ref[...] = jnp.full_like(m_ref, NEG)
     l_ref[...] = jnp.zeros_like(l_ref)
-    score(jnp.int32(0), jnp.int32(0), s0)
+    s1[...] = jnp.zeros_like(s1)
+    p0[...] = jnp.zeros_like(p0)
+    qt[total_items] = jnp.zeros((HEAD, BLOCK), jnp.bfloat16)
+    start = (jnp.int32(0), jnp.int32(0))
+    spare = (jnp.int32(total_items), jnp.int32(0))
 
     def pair(_, state):
-        item0, at0 = state
-        item1, at1 = advance(item0, at0)
-        score(item1, at1, s1)
-        absorb(item0, at0, s0)
-        item2, at2 = advance(item1, at1)
-        score(item2, at2, s0)
-        absorb(item1, at1, s1)
-        return item2, at2
-
-    lax.fori_loop(0, (steps + 1) // 2, pair, (jnp.int32(0), jnp.int32(0)))
+        a, b, c, peak, alpha = state
+        peak0 = score(*a, s0)
+        gather_values(c, alpha, p0)
+        alpha1 = soften(b, peak, s1, p1)
+        d = advance(a)
+        peak1 = score(*d, s1)
+        gather_values(b, alpha1, p1)
+        alpha0 = soften(a, peak0, s0, p0)
+        return advance(d), d, a, peak1, alpha0
+
+    lax.fori_loop(0, (steps + 3) >> 1, pair, (
+        start, spare, spare, jnp.full((1, BLOCK), NEG, jnp.float32), jnp.zeros((1, BLOCK), jnp.float32)))
 
 
 def attend(blocks, counts, kv, queries):
@@ -299,15 +315,18 @@
     return pl.pallas_call(
         attend_kernel,
         out_shape=(
-            jax.ShapeDtypeStruct((ITEMS, SLAB, BLOCK), jnp.bfloat16),
-            jax.ShapeDtypeStruct((ITEMS, 8, BLOCK), jnp.float32),
+            jax.ShapeDtypeStruct((ITEMS + 1, SLAB, BLOCK), jnp.bfloat16),
+            jax.ShapeDtypeStruct((ITEMS + 1, 8, BLOCK), jnp.float32),
         ),
         in_specs=[smem, smem, vmem, vmem],
         out_specs=(vmem, vmem),
         scratch_shapes=[
-            pltpu.VMEM((HEADS_HERE, KBLOCKS, HEAD, BLOCK), jnp.bfloat16),
+            pltpu.VMEM((HEADS_HERE * KBLOCKS, HEAD, BLOCK), jnp.bfloat16),
+            pltpu.VMEM((HEADS_HERE * ITEMS + 1, HEAD, BLOCK), jnp.bfloat16),
             pltpu.VMEM((UNROLL * BLOCK, BLOCK), jnp.float32),
             pltpu.VMEM((UNROLL * BLOCK, BLOCK), jnp.float32),
+            pltpu.VMEM((UNROLL * BLOCK, BLOCK), jnp.bfloat16),
+            pltpu.VMEM((UNROLL * BLOCK, BLOCK), jnp.bfloat16),
             pltpu.VMEM((HEAD, BLOCK), jnp.float32),
             pltpu.VMEM((1, BLOCK), jnp.float32),
             pltpu.VMEM((1, BLOCK), jnp.float32),
@@ -337,13 +356,13 @@
     for d in (2, 1, 3):
         xd = (x + d) % NX
         dev = device(xd, y, z, c)
-        sends.append(remote(stat_in.at[xd], stat_all.at[x], st_send.at[d], st_recv.at[d], dev))
+        sends.append(remote(stat_in.at[pl.ds(4 * xd, 4)], stat_all.at[x], st_send.at[d], st_recv.at[d], dev))
         sends[-1].start()
         for i in range(4):
-            sends.append(remote(o_in.at[xd, i], o_all.at[x, i], x_send.at[d, i], x_recv.at[d, i], dev))
+            sends.append(remote(o_in.at[4 * xd + i], o_all.at[x, i], x_send.at[d, i], x_recv.at[d, i], dev))
             sends[-1].start()
-    keep_o = pltpu.make_async_copy(o_in.at[x], o_all.at[x], own.at[0])
-    keep_s = pltpu.make_async_copy(stat_in.at[x], stat_all.at[x], own.at[1])
+    keep_o = pltpu.make_async_copy(o_in.at[pl.ds(4 * x, 4)], o_all.at[x], own.at[0])
+    keep_s = pltpu.make_async_copy(stat_in.at[pl.ds(4 * x, 4)], stat_all.at[x], own.at[1])
     keep_o.start()
     keep_s.start()
 
@@ -457,7 +476,7 @@
     hit = allowed[..., None] & (rank[..., None] == spot)
     blocks = jnp.sum(jnp.where(hit, spot[:, None], 0), axis=2)
     counts = jnp.sum(allowed.astype(jnp.int32), axis=2)
-    return blocks.reshape(-1), counts.reshape(-1)
+    return (jnp.pad(blocks.reshape(-1), (0, KBLOCKS)), jnp.pad(counts.reshape(-1), (0, 1)))
 
 
 def per_device(queries, keys, values, block_mask, layout):
@@ -465,7 +484,7 @@
     blocks, counts = block_lists(block_mask, swapped, layout)
     partial, stats = attend(blocks, counts, kv.reshape(KBLOCKS, BLOCK, 2 * SLAB),
                             q.reshape(ITEMS, BLOCK, SLAB))
-    return merge(partial.reshape(NX, 4, SLAB, BLOCK), stats.reshape(NX, 4, 8, BLOCK))
+    return merge(partial, stats)
 
 
 def solution(mesh):

time: 159 us -> 145 us (0.912)
  Pallas kernels: 152 us -> 137 us
    pallas_call x1, Pallas kernels: 60.4 us -> 47.5 us  [attend(): pl.pallas_call(attend_kernel, out_shape=(jax.ShapeDtypeStruct((ITEMS + 1,...]
    pallas_call x1, Pallas kernels: 38.6 us -> 36.9 us  [merge(): pl.pallas_call(merge_kernel, out_shape=jax.ShapeDtypeStruct((HALF, NZ * S...]
where the time goes in v2:
time: 145 us; the launch traced here: 144 us
  Pallas kernels  137 us (94%)
  local copies, waits for them, and re-layouts  3.13 us (2%)
  matrix products  3.08 us (2%)
    pallas_call x1, Pallas kernels, gather(): pl.pallas_call(gather_kernel, out_shape=(jax.ShapeDtypeStruct((NY, NZ, 2,...  52.9 us
    pallas_call x1, Pallas kernels, attend(): pl.pallas_call(attend_kernel, out_shape=(jax.ShapeDtypeStruct((ITEMS + 1,...  47.5 us
    pallas_call x1, Pallas kernels, merge(): pl.pallas_call(merge_kernel, out_shape=jax.ShapeDtypeStruct((HALF, NZ * S...  36.9 us

profile of v2, /device:TPU:25, one launch (start us, length us, event | category | flops | bytes accessed | tf_op | source)
XLA Modules:
  0.0 144.3 jit_solution(9333725032835297231)
XLA Ops:
  0.0 0.0 copy-start
  0.0 0.9 fusion.5
  0.9 0.9 fusion.4
  1.8 52.9 %gather.1 = (bf16[4,8,2,64,768]{4,3,2,1,0:T(8,128)(2,1)}, bf16[4,4,2,64,384]{4,3,2,1,0:T(8,128)(2,1)}, s32[3,128,128]{2,1,0:T(8,128)}) custom-call(bf16[64,3072]{1,0:T(8,128)(2,1)} %q_in.1, bf16[64,3072]{1,0:T(8,128)(2,1)} %k_in.1, bf16[64,3072]{1,0:T(8,128)(2,1)} %v_in.1, s32[3,128,128]{2,1,0:T(8,128)} %mask_in.1), custom_call_target="tpu_custom_call" | custom-call | tf_op jit(solution)/shard_map/gather/pallas_call | solution.py:198
  54.7 0.0 copy-done
  54.7 1.2 fusion.6
  55.9 0.1 convert_reduce_fusion
  56.0 0.1 reshape.45
  56.1 0.6 pad.9.counts
  56.7 0.1 convolution_convert_fusion
  56.9 0.6 select_reduce_fusion
  57.4 0.1 reshape.44
  57.5 0.6 pad.8.blocks
  58.1 47.5 %attend.1 = (bf16[17,384,128]{2,1,0:T(8,128)(2,1)}, f32[17,8,128]{2,1,0:T(8,128)}) custom-call(s32[1568]{0:T(1024)} %pad.8.blocks, s32[49]{0:T(128)} %pad.9.counts, bf16[32,128,768]{2,1,0:T(8,128)(2,1)} %bitcast.18, bf16[16,128,384]{2,1,0:T(8,128)(2,1)} %bitcast.19), custom_call_target="tpu_custom_call" | custom-call | tf_op jit(solution)/shard_map/attend/pallas_call | solution.py:315
  105.6 36.9 %merge.1 = bf16[64,3072]{1,0:T(8,128)(2,1)} custom-call(bf16[17,384,128]{2,1,0:T(8,128)(2,1)} %get-tuple-element.13.o_in, f32[17,8,128]{2,1,0:T(8,128)} %get-tuple-element.14.stat_in), custom_call_target="tpu_custom_call" | custom-call | tf_op jit(solution)/shard_map/merge/pallas_call | solution.py:439
  142.5 1.8 %copy.7 = bf16[64,3072]{1,0:T(8,128)(2,1)} copy(bf16[64,3072]{1,0:T(8,128)(2,1)} %merge.1) | data formatting | bytes 786432
  (3 shorter events, 0.0 us)
Async XLA Ops:
  0.0 54.7 %copy-start = (s32[3,128,128]{2,1,0:T(8,128)S(1)}, s32[3,128,128]{2,1,0:T(8,128)}, u32[]{:S(2)}) copy-start(s32[3,128,128]{2,1,0:T(8,128)} %mask_in.1) | copy-start | bytes 589828

commit v3 on v2

--- a/solution.py
+++ b/solution.py
@@ -16,6 +16,7 @@
 ITEMS = NX * (NZ // 2)
 KBLOCKS = NY * NZ
 UNROLL = 4
+WIDE = 2
 NEG = -1e30
 BIG = 1e30
 COEF = math.log2(math.e) / math.sqrt(HEAD)
@@ -136,7 +137,13 @@
             start(remote(piece, piece, s_send.at[1 + way, d], s_recv.at[1 + way, d],
                          device(x, y, z, other)))
 
-    def spread_q(i):
+    odd = (z + c) % 2
+    q_order = []
+    for even_d, odd_d in zip((0, 2, 6, 4), (1, 7, 3, 5)):
+        q_order.append(((z - even_d - odd * (odd_d - even_d) + NZ) % NZ) // 2)
+
+    def spread_q(k):
+        i = q_order[k]
         for cc in range(2):
             piece = q.at[x, i, cc]
             local = (c == parity) & (i == half) & (c == cc)
@@ -150,15 +157,15 @@
                 waiter(piece, q_recv.at[i, cc]).wait_recv()
 
         piece = q.at[x, i]
-        start(remote(piece, piece, x_send.at[0, i], x_recv.at[0, i], device(xn, y, z, c)))
-        start(remote(piece, piece, x_send.at[1, i], x_recv.at[1, i], device(xp, y, z, c)))
-
-    def relay_q(i):
+        start(remote(piece, piece, x_send.at[0, k], x_recv.at[0, k], device(xn, y, z, c)))
+        start(remote(piece, piece, x_send.at[1, k], x_recv.at[1, k], device(xp, y, z, c)))
+
+    def relay_q(k):
         for way, (row, ahead) in enumerate(((xp, xn), (xn, xp))):
-            piece = q.at[row, i]
-            waiter(piece, x_recv.at[way, i]).wait_recv()
-            if i % 2 == way:
-                start(remote(piece, piece, xf_send.at[i], xf_recv.at[i], device(ahead, y, z, c)))
+            piece = q.at[row, q_order[k]]
+            waiter(piece, x_recv.at[way, k]).wait_recv()
+            if k % 2 == way:
+                start(remote(piece, piece, xf_send.at[k], xf_recv.at[k], device(ahead, y, z, c)))
 
     seq = (0,) + ORDER
     for step in range(len(seq) + 2):
@@ -166,17 +173,17 @@
             spread(seq[step])
         if step >= 2:
             relay(seq[step - 2])
-    for i in range(4):
-        spread_q(i)
+        if step % 2 and step < len(seq):
+            spread_q(step // 2)
+        if step in (4, 6, 8, 9):
+            relay_q((4, 6, 8, 9).index(step))
     for d in seq:
         zs = (z - d + NZ) % NZ
         piece = kv.at[y2, zs, c]
         waiter(piece, f_recv.at[d]).wait_recv()
         start(remote(piece, piece, s_send.at[3, d], s_recv.at[3, d], device(x, y, z, other)))
-    for i in range(4):
-        relay_q(i)
-    for i in range(4):
-        waiter(q.at[x2, i], xf_recv.at[i]).wait_recv()
+    for k in range(4):
+        waiter(q.at[x2, q_order[k]], xf_recv.at[k]).wait_recv()
     for d in seq:
         zs = (z - d + NZ) % NZ
         for slot, row in enumerate((y, yp, yn, y2)):
@@ -215,17 +222,44 @@
     )(queries, keys, values, block_mask)
 
 
-def attend_kernel(blocks, counts, kv_ref, q_ref, o_ref, stat_ref, vt, qt, s0, s1, p0, p1, acc, m_ref, l_ref):
+def attend_kernel(blocks, counts, kv_in, q_in, o_ref, stat_ref, kv_ref, q_ref, vt, qt, s_ref, p_ref, acc, m_ref,
+                  l_ref, sems):
     total_items = HEADS_HERE * ITEMS
 
+    copies = []
     for head in range(HEADS_HERE):
-        @pl.loop(0, KBLOCKS)
+        k_cols, v_cols = pl.ds(head * HEAD, HEAD), pl.ds(SLAB + head * HEAD, HEAD)
+        copies.append((
+            pltpu.make_async_copy(kv_in.at[:, :, v_cols], kv_ref.at[:, :, v_cols], sems.at[head, 0]),
+            pltpu.make_async_copy(q_in.at[:, :, k_cols], q_ref.at[:, :, k_cols], sems.at[head, 1]),
+            pltpu.make_async_copy(kv_in.at[:, :, k_cols], kv_ref.at[:, :, k_cols], sems.at[head, 2])))
+        for copy in copies[-1]:
+            copy.start()
+
+    acc[...] = jnp.zeros_like(acc)
+    m_ref[...] = jnp.full_like(m_ref, NEG)
+    l_ref[...] = jnp.zeros_like(l_ref)
+    s_ref[...] = jnp.zeros_like(s_ref)
+    p_ref[...] = jnp.zeros_like(p_ref)
+    qt[total_items] = jnp.zeros((HEAD, BLOCK), jnp.bfloat16)
+
+    for head in range(HEADS_HERE):
+        copies[head][0].wait()
+
+        @pl.loop(0, KBLOCKS, step=4)
         def _(b, head=head):
-            vt[head * KBLOCKS + b] = kv_ref[b, :, SLAB + head * HEAD:SLAB + (head + 1) * HEAD].T
-
-        @pl.loop(0, ITEMS)
+            for u in range(4):
+                vt[head * KBLOCKS + b + u] = kv_ref[b + u, :, SLAB + head * HEAD:SLAB + (head + 1) * HEAD].T
+
+        copies[head][1].wait()
+
+        @pl.loop(0, ITEMS, step=4)
         def _(i, head=head):
-            qt[head * ITEMS + i] = q_ref[i, :, head * HEAD:(head + 1) * HEAD].T
+            for u in range(4):
+                qt[head * ITEMS + i + u] = q_ref[i + u, :, head * HEAD:(head + 1) * HEAD].T
+
+    for head in range(HEADS_HERE):
+        copies[head][2].wait()
 
     def steps_of(item):
         return jnp.maximum((counts[item] + UNROLL - 1) >> 2, 1)
@@ -285,51 +319,49 @@
         done = at + UNROLL >= counts[item]
         return jnp.minimum(jnp.where(done, item + 1, item), total_items), jnp.where(done, 0, at + UNROLL)
 
-    acc[...] = jnp.zeros_like(acc)
-    m_ref[...] = jnp.full_like(m_ref, NEG)
-    l_ref[...] = jnp.zeros_like(l_ref)
-    s1[...] = jnp.zeros_like(s1)
-    p0[...] = jnp.zeros_like(p0)
-    qt[total_items] = jnp.zeros((HEAD, BLOCK), jnp.bfloat16)
     start = (jnp.int32(0), jnp.int32(0))
     spare = (jnp.int32(total_items), jnp.int32(0))
 
-    def pair(_, state):
-        a, b, c, peak, alpha = state
-        peak0 = score(*a, s0)
-        gather_values(c, alpha, p0)
-        alpha1 = soften(b, peak, s1, p1)
-        d = advance(a)
-        peak1 = score(*d, s1)
-        gather_values(b, alpha1, p1)
-        alpha0 = soften(a, peak0, s0, p0)
-        return advance(d), d, a, peak1, alpha0
-
-    lax.fori_loop(0, (steps + 3) >> 1, pair, (
-        start, spare, spare, jnp.full((1, BLOCK), NEG, jnp.float32), jnp.zeros((1, BLOCK), jnp.float32)))
+    def group_step(_, state):
+        at, chunks_b, chunks_c, peaks, alphas = state
+        chunks_a = []
+        for _ in range(WIDE):
+            chunks_a.append(at)
+            at = advance(at)
+        for w in range(WIDE):
+            gather_values(chunks_c[w], alphas[w], p_ref.at[w])
+        alphas = [soften(chunks_b[w], peaks[w], s_ref.at[w], p_ref.at[w]) for w in range(WIDE)]
+        peaks = [score(*chunks_a[w], s_ref.at[w]) for w in range(WIDE)]
+        return at, tuple(chunks_a), chunks_b, tuple(peaks), tuple(alphas)
+
+    lax.fori_loop(0, (steps + WIDE - 1) // WIDE + 2, group_step, (
+        start, (spare,) * WIDE, (spare,) * WIDE,
+        (jnp.full((1, BLOCK), NEG, jnp.float32),) * WIDE, (jnp.zeros((1, BLOCK), jnp.float32),) * WIDE))
 
 
 def attend(blocks, counts, kv, queries):
     vmem = pl.BlockSpec(memory_space=pltpu.VMEM)
     smem = pl.BlockSpec(memory_space=pltpu.SMEM)
+    any_space = pl.BlockSpec(memory_space=pl.ANY)
     return pl.pallas_call(
         attend_kernel,
         out_shape=(
             jax.ShapeDtypeStruct((ITEMS + 1, SLAB, BLOCK), jnp.bfloat16),
             jax.ShapeDtypeStruct((ITEMS + 1, 8, BLOCK), jnp.float32),
         ),
-        in_specs=[smem, smem, vmem, vmem],
+        in_specs=[smem, smem, any_space, any_space],
         out_specs=(vmem, vmem),
         scratch_shapes=[
+            pltpu.VMEM((KBLOCKS, BLOCK, 2 * SLAB), jnp.bfloat16),
+            pltpu.VMEM((ITEMS, BLOCK, SLAB), jnp.bfloat16),
             pltpu.VMEM((HEADS_HERE * KBLOCKS, HEAD, BLOCK), jnp.bfloat16),
             pltpu.VMEM((HEADS_HERE * ITEMS + 1, HEAD, BLOCK), jnp.bfloat16),
-            pltpu.VMEM((UNROLL * BLOCK, BLOCK), jnp.float32),
-            pltpu.VMEM((UNROLL * BLOCK, BLOCK), jnp.float32),
-            pltpu.VMEM((UNROLL * BLOCK, BLOCK), jnp.bfloat16),
-            pltpu.VMEM((UNROLL * BLOCK, BLOCK), jnp.bfloat16),
+            pltpu.VMEM((WIDE, UNROLL * BLOCK, BLOCK), jnp.float32),
+            pltpu.VMEM((WIDE, UNROLL * BLOCK, BLOCK), jnp.bfloat16),
             pltpu.VMEM((HEAD, BLOCK), jnp.float32),
             pltpu.VMEM((1, BLOCK), jnp.float32),
             pltpu.VMEM((1, BLOCK), jnp.float32),
+            pltpu.SemaphoreType.DMA((HEADS_HERE, 3)),
         ],
         name="attend",
     )(blocks, counts, kv, queries)
@@ -353,12 +385,13 @@
     pl.semaphore_wait(barrier, len(peers))
 
     sends = []
-    for d in (2, 1, 3):
-        xd = (x + d) % NX
-        dev = device(xd, y, z, c)
-        sends.append(remote(stat_in.at[pl.ds(4 * xd, 4)], stat_all.at[x], st_send.at[d], st_recv.at[d], dev))
-        sends[-1].start()
-        for i in range(4):
+    for i in range(4):
+        for d in (2, 1, 3):
+            xd = (x + d) % NX
+            dev = device(xd, y, z, c)
+            if i == 0:
+                sends.append(remote(stat_in.at[pl.ds(4 * xd, 4)], stat_all.at[x], st_send.at[d], st_recv.at[d], dev))
+                sends[-1].start()
             sends.append(remote(o_in.at[4 * xd + i], o_all.at[x, i], x_send.at[d, i], x_recv.at[d, i], dev))
             sends[-1].start()
     keep_o = pltpu.make_async_copy(o_in.at[pl.ds(4 * x, 4)], o_all.at[x], own.at[0])
@@ -408,8 +441,9 @@
             w = [jnp.exp2(v - top) for v in m]
             total = sum(w[s] * stat_all[s, i, 2 * head + 1:2 * head + 2, :] for s in range(NX))
             rows = slice(head * HEAD, (head + 1) * HEAD)
-            value = sum(o_all[s, i, rows, :].astype(jnp.float32) * w[s] for s in range(NX))
-            result[i, :, rows] = (value / total).T.astype(jnp.bfloat16)
+            share = 1.0 / total
+            value = sum(o_all[s, i, rows, :].astype(jnp.float32) * (w[s] * share) for s in range(NX))
+            result[i, :, rows] = value.T.astype(jnp.bfloat16)
         if i:
             ship(i - 1)
     ship(3)

time: 145 us -> 126 us (0.87)
  Pallas kernels: 137 us -> 119 us
    pallas_call x1, Pallas kernels: 47.5 us -> 36.6 us  [attend(): pl.pallas_call(attend_kernel, out_shape=(jax.ShapeDtypeStruct((ITEMS + 1,...]
    pallas_call x1, Pallas kernels: 52.9 us -> 46.1 us  [gather(): pl.pallas_call(gather_kernel, out_shape=(jax.ShapeDtypeStruct((NY, NZ, 2,...]
where the time goes in v3:
time: 126 us
  Pallas kernels  119 us (94%)
  local copies, waits for them, and re-layouts  3.13 us (2%)
  matrix products  3.08 us (2%)
    pallas_call x1, Pallas kernels, gather(): pl.pallas_call(gather_kernel, out_shape=(jax.ShapeDtypeStruct((NY, NZ, 2,...  46.1 us
    pallas_call x1, Pallas kernels, attend(): pl.pallas_call(attend_kernel, out_shape=(jax.ShapeDtypeStruct((ITEMS + 1,...  36.6 us
    pallas_call x1, Pallas kernels, merge(): pl.pallas_call(merge_kernel, out_shape=jax.ShapeDtypeStruct((HALF, NZ * S...  36.5 us

profile of v3, /device:TPU:25, one launch (start us, length us, event | category | flops | bytes accessed | tf_op | source)
XLA Modules:
  0.0 126.2 jit_solution(14393209869580821989)
XLA Ops:
  0.0 0.0 copy-start
  0.0 0.9 fusion.5
  0.9 0.9 fusion.4
  1.8 46.1 %gather.1 = (bf16[4,8,2,64,768]{4,3,2,1,0:T(8,128)(2,1)}, bf16[4,4,2,64,384]{4,3,2,1,0:T(8,128)(2,1)}, s32[3,128,128]{2,1,0:T(8,128)}) custom-call(bf16[64,3072]{1,0:T(8,128)(2,1)} %q_in.1, bf16[64,3072]{1,0:T(8,128)(2,1)} %k_in.1, bf16[64,3072]{1,0:T(8,128)(2,1)} %v_in.1, s32[3,128,128]{2,1,0:T(8,128)} %mask_in.1), custom_call_target="tpu_custom_call" | custom-call | tf_op jit(solution)/shard_map/gather/pallas_call | solution.py:205
  47.9 0.0 copy-done
  47.9 1.2 fusion.6
  49.1 0.1 convert_reduce_fusion
  49.2 0.1 reshape.45
  49.3 0.6 pad.9.counts
  49.9 0.1 convolution_convert_fusion
  50.1 0.6 select_reduce_fusion
  50.6 0.1 reshape.44
  50.7 0.6 pad.8.blocks
  51.3 36.6 %attend.1 = (bf16[17,384,128]{2,1,0:T(8,128)(2,1)}, f32[17,8,128]{2,1,0:T(8,128)}) custom-call(s32[1568]{0:T(1024)} %pad.8.blocks, s32[49]{0:T(128)} %pad.9.counts, bf16[32,128,768]{2,1,0:T(8,128)(2,1)} %bitcast.18, bf16[16,128,384]{2,1,0:T(8,128)(2,1)} %bitcast.19), custom_call_target="tpu_custom_call" | custom-call | tf_op jit(solution)/shard_map/attend/pallas_call | solution.py:346
  87.9 36.5 %merge.1 = bf16[64,3072]{1,0:T(8,128)(2,1)} custom-call(bf16[17,384,128]{2,1,0:T(8,128)(2,1)} %get-tuple-element.13.o_in, f32[17,8,128]{2,1,0:T(8,128)} %get-tuple-element.14.stat_in), custom_call_target="tpu_custom_call" | custom-call | tf_op jit(solution)/shard_map/merge/pallas_call | solution.py:473
  124.4 1.8 %copy.7 = bf16[64,3072]{1,0:T(8,128)(2,1)} copy(bf16[64,3072]{1,0:T(8,128)(2,1)} %merge.1) | data formatting | bytes 786432
  (3 shorter events, 0.0 us)
Async XLA Ops:
  0.0 47.9 %copy-start = (s32[3,128,128]{2,1,0:T(8,128)S(1)}, s32[3,128,128]{2,1,0:T(8,128)}, u32[]{:S(2)}) copy-start(s32[3,128,128]{2,1,0:T(8,128)} %mask_in.1) | copy-start | bytes 589828

commit v4 on v3

--- a/solution.py
+++ b/solution.py
@@ -15,6 +15,7 @@
 SLAB = HEADS_HERE * HEAD
 ITEMS = NX * (NZ // 2)
 KBLOCKS = NY * NZ
+LIST_ROWS = HEADS_HERE * ITEMS + 8
 UNROLL = 4
 WIDE = 2
 NEG = -1e30
@@ -38,12 +39,49 @@
     return (z % 4) * 2 + z // 4
 
 
-def gather_kernel(q_in, k_in, v_in, mask_in, kv, q, mask,
+def list_blocks(x, y, mask_in, layout_in, tables):
+    shape = (BLOCK, BLOCK)
+    down = lax.broadcasted_iota(jnp.int32, shape, 0)
+    across = lax.broadcasted_iota(jnp.int32, shape, 1)
+
+    def ones(hit):
+        return jnp.where(hit, 1.0, 0.0).astype(jnp.bfloat16)
+
+    def matmul(a, b):
+        return jnp.dot(a, b, preferred_element_type=jnp.float32)
+
+    held = ones(down == jnp.broadcast_to(layout_in[...], shape))
+    stored_row = 32 * ((across >> 2) & 3) + 8 * y + 2 * (across & 3) + (across >> 4)
+    rows = matmul(held, ones((down == stored_row) & (across < 2 * ITEMS))).T.astype(jnp.bfloat16)
+    cols = matmul(held, ones((down == 32 * x + across) & (across < KBLOCKS))).astype(jnp.bfloat16)
+    before = ones(down < across)
+    lane = lax.broadcasted_iota(jnp.int32, (2 * ITEMS, BLOCK), 1)
+    for head in range(HEADS_HERE):
+        mask = mask_in[head].astype(jnp.float32).astype(jnp.bfloat16)
+        some = matmul(rows, mask).astype(jnp.bfloat16)
+        allowed = matmul(some, cols)
+        rank = matmul(allowed.astype(jnp.bfloat16), before)[:2 * ITEMS]
+        allowed = allowed[:2 * ITEMS]
+        slot = jnp.where(allowed > 0.5, rank, -1.0)
+        number = lane.astype(jnp.float32)
+        table = jnp.where(lane == KBLOCKS, jnp.sum(allowed, axis=1, keepdims=True), 0.0)
+        for p in range(KBLOCKS):
+            found = jnp.sum(jnp.where(slot == float(p), number, 0.0), axis=1, keepdims=True)
+            table = jnp.where(lane == p, found, table)
+        table = table.astype(jnp.int32)
+        for part in range(2):
+            tables[part, head * ITEMS:(head + 1) * ITEMS] = table[part * ITEMS:(part + 1) * ITEMS]
+    for part in range(2):
+        tables[part, HEADS_HERE * ITEMS:] = jnp.zeros((8, BLOCK), jnp.int32)
+
+
+def gather_kernel(qkv_in, mask_in, layout_in, kv, q, chosen,
                   zs_send, z_recv, q_send, q_recv, y_send, y_recv, f_send, f_recv,
-                  s_send, s_recv, x_send, x_recv, xf_send, xf_recv, own, mask_sem):
+                  s_send, s_recv, x_send, x_recv, xf_send, xf_recv, own, mask_sem, tables, mask_ref, layout_ref):
     x, y, z, c = place()
     other = 1 - c
     parity = z % 2
+    q_in, k_in, v_in = (qkv_in.at[pl.ds(n * HALF, HALF)] for n in range(3))
     yn, yp = (y + 1) % NY, (y + NY - 1) % NY
     xn, xp = (x + 1) % NX, (x + NX - 1) % NX
     y2, x2 = (y + 2) % NY, (x + 2) % NX
@@ -53,6 +91,10 @@
             src_ref=src, dst_ref=dst, send_sem=send, recv_sem=recv,
             device_id=dev, device_id_type=MESH)
 
+    mask_copy = pltpu.make_async_copy(mask_in, mask_ref, own.at[3])
+    layout_copy = pltpu.make_async_copy(layout_in, layout_ref, own.at[4])
+    mask_copy.start()
+    layout_copy.start()
     barrier = pltpu.get_barrier_semaphore()
     peers = [device(x, y, (z + d) % NZ, cc) for d in range(1, NZ) for cc in range(2)]
     peers += [device(x, y, z, other), device(x, yn, z, c), device(x, yp, z, c),
@@ -108,8 +150,9 @@
     def _():
         own_q_copies()[1].start()
 
-    swap = remote(mask_in, mask, mask_sem.at[0], mask_sem.at[1], device(x, y, z, other))
-    swap.start()
+    mask_copy.wait()
+    layout_copy.wait()
+    list_blocks(x, y, mask_ref, layout_ref, tables)
 
     def waiter(dst, recv):
         return remote(dst, dst, recv, recv, device(x, y, z, other))
@@ -184,11 +227,31 @@
         start(remote(piece, piece, s_send.at[3, d], s_recv.at[3, d], device(x, y, z, other)))
     for k in range(4):
         waiter(q.at[x2, q_order[k]], xf_recv.at[k]).wait_recv()
+    def give():
+        return remote(tables.at[other], chosen, mask_sem.at[0], mask_sem.at[1], device(x, y, z, other))
+
+    def keep():
+        return pltpu.make_async_copy(tables.at[c], chosen, mask_sem.at[2])
+
+    @pl.when(c == z // 4)
+    def _():
+        give().start()
+        keep().start()
+
     for d in seq:
         zs = (z - d + NZ) % NZ
         for slot, row in enumerate((y, yp, yn, y2)):
             waiter(kv.at[row, zs, other], s_recv.at[slot, d]).wait_recv()
-    swap.wait()
+
+    @pl.when(c == z // 4)
+    def _():
+        give().wait_send()
+        keep().wait()
+
+    @pl.when(c != z // 4)
+    def _():
+        give().wait_recv()
+
 
     @pl.when(c != parity)
     def _():
@@ -198,43 +261,42 @@
         copy.wait_send()
 
 
-def gather(queries, keys, values, block_mask):
+def gather(queries, keys, values, block_mask, layout):
     any_space = pl.BlockSpec(memory_space=pl.ANY)
-    vmem = pl.BlockSpec(memory_space=pltpu.VMEM)
+    hbm = pl.BlockSpec(memory_space=pltpu.HBM)
     dma = pltpu.SemaphoreType.DMA
     return pl.pallas_call(
         gather_kernel,
         out_shape=(
             jax.ShapeDtypeStruct((NY, NZ, 2, HALF, 2 * SLAB), jnp.bfloat16),
             jax.ShapeDtypeStruct((NX, NZ // 2, 2, HALF, SLAB), jnp.bfloat16),
-            jax.ShapeDtypeStruct(block_mask.shape, block_mask.dtype),
+            jax.ShapeDtypeStruct((LIST_ROWS, BLOCK), jnp.int32),
         ),
-        in_specs=[vmem, vmem, vmem, any_space],
+        in_specs=[hbm] * 3,
         out_specs=(any_space, any_space, any_space),
         scratch_shapes=[
             dma((2, NZ)), dma((2, NZ)), dma((NZ,)), dma((4, 2)),
             dma((2, NZ)), dma((2, NZ)), dma((NZ,)), dma((NZ,)),
             dma((4, NZ)), dma((4, NZ)),
-            dma((2, 4)), dma((2, 4)), dma((4,)), dma((4,)), dma((3,)), dma((2,)),
+            dma((2, 4)), dma((2, 4)), dma((4,)), dma((4,)), dma((5,)), dma((3,)),
+            pltpu.VMEM((2, LIST_ROWS, BLOCK), jnp.int32),
+            pltpu.VMEM((HEADS_HERE, BLOCK, BLOCK), jnp.int32),
+            pltpu.VMEM((1, BLOCK), jnp.int32),
         ],
-        compiler_params=pltpu.CompilerParams(collective_id=0, has_side_effects=True),
+        compiler_params=pltpu.CompilerParams(
+            collective_id=0, has_side_effects=True, vmem_limit_bytes=8 * 1024 * 1024),
         name="gather",
-    )(queries, keys, values, block_mask)
-
-
-def attend_kernel(blocks, counts, kv_in, q_in, o_ref, stat_ref, kv_ref, q_ref, vt, qt, s_ref, p_ref, acc, m_ref,
-                  l_ref, sems):
+    )(jnp.concatenate((queries, keys, values), axis=0), block_mask, layout.reshape(1, -1))
+
+
+def attend_kernel(lists, kv_ref, q_ref, o_ref, stat_ref, vt, qt, s_ref, p_ref, acc, m_ref, l_ref):
     total_items = HEADS_HERE * ITEMS
 
-    copies = []
-    for head in range(HEADS_HERE):
-        k_cols, v_cols = pl.ds(head * HEAD, HEAD), pl.ds(SLAB + head * HEAD, HEAD)
-        copies.append((
-            pltpu.make_async_copy(kv_in.at[:, :, v_cols], kv_ref.at[:, :, v_cols], sems.at[head, 0]),
-            pltpu.make_async_copy(q_in.at[:, :, k_cols], q_ref.at[:, :, k_cols], sems.at[head, 1]),
-            pltpu.make_async_copy(kv_in.at[:, :, k_cols], kv_ref.at[:, :, k_cols], sems.at[head, 2])))
-        for copy in copies[-1]:
-            copy.start()
+    def block(item, column):
+        return lists[item, column]
+
+    def count_of(item):
+        return block(item, KBLOCKS)
 
     acc[...] = jnp.zeros_like(acc)
     m_ref[...] = jnp.full_like(m_ref, NEG)
@@ -244,25 +306,18 @@
     qt[total_items] = jnp.zeros((HEAD, BLOCK), jnp.bfloat16)
 
     for head in range(HEADS_HERE):
-        copies[head][0].wait()
-
         @pl.loop(0, KBLOCKS, step=4)
         def _(b, head=head):
             for u in range(4):
                 vt[head * KBLOCKS + b + u] = kv_ref[b + u, :, SLAB + head * HEAD:SLAB + (head + 1) * HEAD].T
 
-        copies[head][1].wait()
-
         @pl.loop(0, ITEMS, step=4)
         def _(i, head=head):
             for u in range(4):
                 qt[head * ITEMS + i + u] = q_ref[i + u, :, head * HEAD:(head + 1) * HEAD].T
 
-    for head in range(HEADS_HERE):
-        copies[head][2].wait()
-
     def steps_of(item):
-        return jnp.maximum((counts[item] + UNROLL - 1) >> 2, 1)
+        return jnp.maximum((count_of(item) + UNROLL - 1) >> 2, 1)
 
     steps = lax.fori_loop(0, total_items, lambda i, n: n + steps_of(i), 0)
 
@@ -271,10 +326,9 @@
         return jnp.where(spare, ITEMS, item & (ITEMS - 1)), jnp.where(spare, 0, item >> 4)
 
     def score(item, at, out):
-        base = item * KBLOCKS + at
-        left = counts[item] - at
+        left = count_of(item) - at
         cols = pl.ds(pl.multiple_of(home(item)[1] * HEAD, HEAD), HEAD)
-        rows = [kv_ref[blocks[base + u], :, cols] for u in range(UNROLL)]
+        rows = [kv_ref[block(item, at + u), :, cols] for u in range(UNROLL)]
         t = jnp.dot(jnp.concatenate(rows, axis=0), qt[item], preferred_element_type=jnp.float32) * COEF
         out[...] = t
         peak = jnp.full((1, BLOCK), NEG, jnp.float32)
@@ -286,7 +340,7 @@
     def soften(chunk, peak, src, out):
         item, at = chunk
         first = at == 0
-        left = counts[item] - at
+        left = count_of(item) - at
         m_old = jnp.where(first, NEG, m_ref[...])
         m_new = jnp.maximum(m_old, peak)
         alpha = jnp.where(first, 0.0, jnp.exp2(m_old - m_new))
@@ -306,9 +360,8 @@
 
     def gather_values(chunk, alpha, src):
         item, at = chunk
-        base = item * KBLOCKS + at
         where, head = home(item)
-        cols = [vt[head * KBLOCKS + blocks[base + u]] for u in range(UNROLL)]
+        cols = [vt[head * KBLOCKS + block(item, at + u)] for u in range(UNROLL)]
         value = acc[...] * alpha + jnp.dot(jnp.concatenate(cols, axis=1), src[...],
                                            preferred_element_type=jnp.float32)
         acc[...] = value
@@ -316,7 +369,7 @@
 
     def advance(chunk):
         item, at = chunk
-        done = at + UNROLL >= counts[item]
+        done = at + UNROLL >= count_of(item)
         return jnp.minimum(jnp.where(done, item + 1, item), total_items), jnp.where(done, 0, at + UNROLL)
 
     start = (jnp.int32(0), jnp.int32(0))
@@ -339,21 +392,18 @@
         (jnp.full((1, BLOCK), NEG, jnp.float32),) * WIDE, (jnp.zeros((1, BLOCK), jnp.float32),) * WIDE))
 
 
-def attend(blocks, counts, kv, queries):
+def attend(lists, kv, queries):
     vmem = pl.BlockSpec(memory_space=pltpu.VMEM)
     smem = pl.BlockSpec(memory_space=pltpu.SMEM)
-    any_space = pl.BlockSpec(memory_space=pl.ANY)
     return pl.pallas_call(
         attend_kernel,
         out_shape=(
             jax.ShapeDtypeStruct((ITEMS + 1, SLAB, BLOCK), jnp.bfloat16),
             jax.ShapeDtypeStruct((ITEMS + 1, 8, BLOCK), jnp.float32),
         ),
-        in_specs=[smem, smem, any_space, any_space],
+        in_specs=[smem, vmem, vmem],
         out_specs=(vmem, vmem),
         scratch_shapes=[
-            pltpu.VMEM((KBLOCKS, BLOCK, 2 * SLAB), jnp.bfloat16),
-            pltpu.VMEM((ITEMS, BLOCK, SLAB), jnp.bfloat16),
             pltpu.VMEM((HEADS_HERE * KBLOCKS, HEAD, BLOCK), jnp.bfloat16),
             pltpu.VMEM((HEADS_HERE * ITEMS + 1, HEAD, BLOCK), jnp.bfloat16),
             pltpu.VMEM((WIDE, UNROLL * BLOCK, BLOCK), jnp.float32),
@@ -361,10 +411,10 @@
             pltpu.VMEM((HEAD, BLOCK), jnp.float32),
             pltpu.VMEM((1, BLOCK), jnp.float32),
             pltpu.VMEM((1, BLOCK), jnp.float32),
-            pltpu.SemaphoreType.DMA((HEADS_HERE, 3)),
         ],
+        compiler_params=pltpu.CompilerParams(vmem_limit_bytes=24 * 1024 * 1024),
         name="attend",
-    )(blocks, counts, kv, queries)
+    )(lists, kv, queries)
 
 
 def merge_kernel(o_in, stat_in, out, o_all, stat_all, result, x_send, x_recv, st_send, st_recv,
@@ -482,42 +532,15 @@
             dma((NX, 4)), dma((NX, 4)), dma((NX,)), dma((NX,)),
             dma((4, 2)), dma((NZ,)), dma((3,)),
         ],
-        compiler_params=pltpu.CompilerParams(collective_id=1, has_side_effects=True),
+        compiler_params=pltpu.CompilerParams(
+            collective_id=1, has_side_effects=True, vmem_limit_bytes=8 * 1024 * 1024),
         name="merge",
     )(partial, stats)
 
 
-def block_lists(block_mask, swapped, layout):
-    x, y, z, c = place()
-    mask = jnp.where(c == lax.axis_index("zh"), block_mask, swapped)
-    numbers = jnp.arange(KBLOCKS * NX, dtype=jnp.int32)
-    item = jnp.arange(ITEMS, dtype=jnp.int32)
-    rows = 32 * (item // 4) + 8 * y + 2 * (item % 4) + c
-    cols = 32 * x + jnp.arange(KBLOCKS, dtype=jnp.int32)
-    select = layout[:, None] == numbers[None, :]
-
-    def picker(stored):
-        hit = (stored[:, None] == numbers[None, :]).astype(jnp.bfloat16)
-        return jnp.dot(hit, select.astype(jnp.bfloat16), preferred_element_type=jnp.float32).astype(jnp.bfloat16)
-
-    some = jnp.einsum("ic,hcd->hid", picker(rows), mask.astype(jnp.bfloat16),
-                      preferred_element_type=jnp.float32).astype(jnp.bfloat16)
-    allowed = jnp.einsum("hid,kd->hik", some, picker(cols), preferred_element_type=jnp.float32) > 0.5
-    spot = jnp.arange(KBLOCKS, dtype=jnp.int32)
-    before = (spot[:, None] < spot[None, :]).astype(jnp.bfloat16)
-    rank = jnp.einsum("hik,kj->hij", allowed.astype(jnp.bfloat16), before,
-                      preferred_element_type=jnp.float32).astype(jnp.int32)
-    hit = allowed[..., None] & (rank[..., None] == spot)
-    blocks = jnp.sum(jnp.where(hit, spot[:, None], 0), axis=2)
-    counts = jnp.sum(allowed.astype(jnp.int32), axis=2)
-    return (jnp.pad(blocks.reshape(-1), (0, KBLOCKS)), jnp.pad(counts.reshape(-1), (0, 1)))
-
-
 def per_device(queries, keys, values, block_mask, layout):
-    kv, q, swapped = gather(queries, keys, values, block_mask)
-    blocks, counts = block_lists(block_mask, swapped, layout)
-    partial, stats = attend(blocks, counts, kv.reshape(KBLOCKS, BLOCK, 2 * SLAB),
-                            q.reshape(ITEMS, BLOCK, SLAB))
+    kv, q, lists = gather(queries, keys, values, block_mask, layout)
+    partial, stats = attend(lists, kv.reshape(KBLOCKS, BLOCK, 2 * SLAB), q.reshape(ITEMS, BLOCK, SLAB))
     return merge(partial, stats)
 
 

time: 126 us -> 118 us (0.937)
  matrix products: 3.08 us -> 0 us
  local copies, waits for them, and re-layouts: 3.13 us -> 0.76 us
  Pallas kernels: 119 us -> 117 us
    dot_general x4 -> x0, matrix products: 3.08 us -> none  [the longest x2 1.75 us: picker(): jnp.dot(hit, select.astype(jnp.bfloat16), preferred_element_type=jnp.floa...]
    pallas_call x1, Pallas kernels: 36.6 us -> 34.1 us  [attend(): pl.pallas_call(attend_kernel, out_shape=(jax.ShapeDtypeStruct((ITEMS + 1,...]
    concatenate x0 -> x1, other arithmetic: none -> 1.35 us  [gather(): jnp.concatenate((queries, keys, values), axis=0)]
where the time goes in v4:
time: 118 us; the launch traced here: 119 us
  Pallas kernels  117 us (99%)
  other arithmetic  1.35 us (1%)
    pallas_call x1, Pallas kernels, gather(): pl.pallas_call(gather_kernel, out_shape=(jax.ShapeDtypeStruct((NY, NZ, 2,...  47 us
    pallas_call x1, Pallas kernels, merge(): pl.pallas_call(merge_kernel, out_shape=jax.ShapeDtypeStruct((HALF, NZ * S...  35.4 us
    pallas_call x1, Pallas kernels, attend(): pl.pallas_call(attend_kernel, out_shape=(jax.ShapeDtypeStruct((ITEMS + 1,...  34.1 us

profile of v4, /device:TPU:25, one launch (start us, length us, event | category | flops | bytes accessed | tf_op | source)
XLA Modules:
  0.0 118.7 jit_solution(15216127428619064385)
XLA Ops:
  0.0 0.0 copy-start.1
  0.0 0.0 copy-start
  0.0 1.3 %pad_maximum_fusion.qkv_in = bf16[192,3072]{1,0:T(8,128)(2,1)S(1)} fusion(bf16[64,3072]{1,0:T(8,128)(2,1)} %param.7, bf16[64,3072]{1,0:T(8,128)(2,1)} %param.6, bf16[64,3072]{1,0:T(8,128)(2,1)} %param.5), kind=kLoop, calls=%fused_computation | loop fusion | flops 3538944 | bytes 2359296 | tf_op jit(solution)/shard_map/concatenate | solution.py:289
  1.4 0.0 copy-done.1
  1.4 0.0 copy-done
  1.4 47.0 %gather.1 = (bf16[4,8,2,64,768]{4,3,2,1,0:T(8,128)(2,1)S(1)}, bf16[4,4,2,64,384]{4,3,2,1,0:T(8,128)(2,1)S(1)}, s32[56,128]{1,0:T(8,128)S(1)}) custom-call(bf16[192,3072]{1,0:T(8,128)(2,1)S(1)} %pad_maximum_fusion.qkv_in, s32[3,128,128]{2,1,0:T(8,128)S(1)} %copy-done, s32[1,128]{1,0:T(1,128)S(1)} %bitcast.5), custom_call_target="tpu_custom_call" | custom-call | tf_op jit(solution)/shard_map/gather/pallas_call | solution.py:268
  48.4 34.1 %attend.1 = (bf16[17,384,128]{2,1,0:T(8,128)(2,1)S(1)}, f32[17,8,128]{2,1,0:T(8,128)S(1)}) custom-call(s32[56,128]{1,0:T(8,128)S(1)} %get-tuple-element.10.lists, bf16[32,128,768]{2,1,0:T(8,128)(2,1)S(1)} %bitcast.3, bf16[16,128,384]{2,1,0:T(8,128)(2,1)S(1)} %bitcast.4), custom_call_target="tpu_custom_call" | custom-call | tf_op jit(solution)/shard_map/attend/pallas_call | solution.py:398
  82.5 35.4 %merge.1 = bf16[64,3072]{1,0:T(8,128)(2,1)S(1)} custom-call(bf16[17,384,128]{2,1,0:T(8,128)(2,1)S(1)} %get-tuple-element.13.o_in, f32[17,8,128]{2,1,0:T(8,128)S(1)} %get-tuple-element.14.stat_in), custom_call_target="tpu_custom_call" | custom-call | tf_op jit(solution)/shard_map/merge/pallas_call | solution.py:523
  117.9 0.7 copy.7
Async XLA Ops:
  0.0 1.4 %copy-start.1 = (s32[128]{0:T(128)S(1)}, s32[128]{0:T(128)}, u32[]{:S(2)}) copy-start(s32[128]{0:T(128)} %param.9) | copy-start | bytes 1540
  0.0 1.4 %copy-start = (s32[3,128,128]{2,1,0:T(8,128)S(1)}, s32[3,128,128]{2,1,0:T(8,128)}, u32[]{:S(2)}) copy-start(s32[3,128,128]{2,1,0:T(8,128)} %mask_in.1) | copy-start | bytes 589828

commit v5 on v4

--- a/solution.py
+++ b/solution.py
@@ -75,13 +75,12 @@
         tables[part, HEADS_HERE * ITEMS:] = jnp.zeros((8, BLOCK), jnp.int32)
 
 
-def gather_kernel(qkv_in, mask_in, layout_in, kv, q, chosen,
+def gather_kernel(q_in, k_in, v_in, mask_in, layout_in, kv, q, chosen,
                   zs_send, z_recv, q_send, q_recv, y_send, y_recv, f_send, f_recv,
                   s_send, s_recv, x_send, x_recv, xf_send, xf_recv, own, mask_sem, tables, mask_ref, layout_ref):
     x, y, z, c = place()
     other = 1 - c
     parity = z % 2
-    q_in, k_in, v_in = (qkv_in.at[pl.ds(n * HALF, HALF)] for n in range(3))
     yn, yp = (y + 1) % NY, (y + NY - 1) % NY
     xn, xp = (x + 1) % NX, (x + NX - 1) % NX
     y2, x2 = (y + 2) % NY, (x + 2) % NX
@@ -272,7 +271,7 @@
             jax.ShapeDtypeStruct((NX, NZ // 2, 2, HALF, SLAB), jnp.bfloat16),
             jax.ShapeDtypeStruct((LIST_ROWS, BLOCK), jnp.int32),
         ),
-        in_specs=[hbm] * 3,
+        in_specs=[hbm] * 5,
         out_specs=(any_space, any_space, any_space),
         scratch_shapes=[
             dma((2, NZ)), dma((2, NZ)), dma((NZ,)), dma((4, 2)),
@@ -286,7 +285,8 @@
         compiler_params=pltpu.CompilerParams(
             collective_id=0, has_side_effects=True, vmem_limit_bytes=8 * 1024 * 1024),
         name="gather",
-    )(jnp.concatenate((queries, keys, values), axis=0), block_mask, layout.reshape(1, -1))
+    )(*(pltpu.with_memory_space_constraint(a, pltpu.HBM)
+        for a in (queries, keys, values, block_mask, layout.reshape(1, -1))))
 
 
 def attend_kernel(lists, kv_ref, q_ref, o_ref, stat_ref, vt, qt, s_ref, p_ref, acc, m_ref, l_ref):
@@ -434,68 +434,75 @@
         pl.semaphore_signal(barrier, inc=1, device_id=peer, device_id_type=MESH)
     pl.semaphore_wait(barrier, len(peers))
 
+    shift = (2, 1, 3, 0)
+    rows_of = [(z // 2 + r) % 4 for r in shift]
     sends = []
-    for i in range(4):
+    for k in range(4):
         for d in (2, 1, 3):
             xd = (x + d) % NX
             dev = device(xd, y, z, c)
-            if i == 0:
+            if k == 0:
                 sends.append(remote(stat_in.at[pl.ds(4 * xd, 4)], stat_all.at[x], st_send.at[d], st_recv.at[d], dev))
                 sends[-1].start()
-            sends.append(remote(o_in.at[4 * xd + i], o_all.at[x, i], x_send.at[d, i], x_recv.at[d, i], dev))
+            sends.append(remote(o_in.at[4 * xd + rows_of[k]], o_all.at[x, k], x_send.at[d, k], x_recv.at[d, k], dev))
             sends[-1].start()
-    keep_o = pltpu.make_async_copy(o_in.at[pl.ds(4 * x, 4)], o_all.at[x], own.at[0])
-    keep_s = pltpu.make_async_copy(stat_in.at[pl.ds(4 * x, 4)], stat_all.at[x], own.at[1])
-    keep_o.start()
-    keep_s.start()
+    keep = [pltpu.make_async_copy(o_in.at[4 * x + rows_of[k]], o_all.at[x, k], own.at[k]) for k in range(4)]
+    keep.append(pltpu.make_async_copy(stat_in.at[pl.ds(4 * x, 4)], stat_all.at[x], own.at[4]))
+    for copy in keep:
+        copy.start()
 
     def waiter(dst, recv):
         return remote(dst, dst, recv, recv, device(x, y, z, other))
 
-    keep_s.wait()
-    keep_o.wait()
+    for copy in keep:
+        copy.wait()
     for d in (1, 3, 2):
         waiter(stat_all.at[(x - d + NX) % NX], st_recv.at[d]).wait_recv()
 
     def columns(zd):
         return pl.ds(pl.multiple_of(group(zd) * SLAB, SLAB), SLAB)
 
-    def local_of(i, cc):
-        src = result.at[i, pl.ds(cc * HALF, HALF)]
-        return pltpu.make_async_copy(src, out.at[:, columns(z)], own.at[2])
-
-    def remote_of(i, cc):
-        src = result.at[i, pl.ds(cc * HALF, HALF)]
-        return remote(src, out.at[:, columns(z)], z_send.at[i, cc], z_recv.at[z],
-                      device(x, y, 2 * i + c, cc))
-
-    def is_local(i, cc):
-        return (2 * i + c == z) & (c == cc)
-
-    def ship(i):
+    def local_of(k, cc):
+        src = result.at[k, pl.ds(cc * HALF, HALF)]
+        return pltpu.make_async_copy(src, out.at[:, columns(z)], own.at[5])
+
+    def remote_of(k, cc):
+        src = result.at[k, pl.ds(cc * HALF, HALF)]
+        return remote(src, out.at[:, columns(z)], z_send.at[k, cc], z_recv.at[z],
+                      device(x, y, 2 * rows_of[k] + c, cc))
+
+    def deliver(k, act_local, act_remote):
         for cc in range(2):
-            @pl.when(is_local(i, cc))
-            def _():
-                local_of(i, cc).start()
-
-            @pl.when(jnp.logical_not(is_local(i, cc)))
-            def _():
-                remote_of(i, cc).start()
-
-    for i in range(4):
+            if shift[k]:
+                act_remote(remote_of(k, cc))
+                continue
+            here = (z % 2 == c) & (c == cc)
+
+            @pl.when(here)
+            def _(cc=cc):
+                act_local(local_of(k, cc))
+
+            @pl.when(jnp.logical_not(here))
+            def _(cc=cc):
+                act_remote(remote_of(k, cc))
+
+    def ship(k):
+        deliver(k, lambda copy: copy.start(), lambda copy: copy.start())
+
+    for k in range(4):
         for d in (1, 3, 2):
-            waiter(o_all.at[(x - d + NX) % NX, i], x_recv.at[d, i]).wait_recv()
+            waiter(o_all.at[(x - d + NX) % NX, k], x_recv.at[d, k]).wait_recv()
         for head in range(HEADS_HERE):
-            m = [stat_all[s, i, 2 * head:2 * head + 1, :] for s in range(NX)]
+            m = [stat_all[s, rows_of[k], 2 * head:2 * head + 1, :] for s in range(NX)]
             top = jnp.maximum(jnp.maximum(m[0], m[1]), jnp.maximum(m[2], m[3]))
             w = [jnp.exp2(v - top) for v in m]
-            total = sum(w[s] * stat_all[s, i, 2 * head + 1:2 * head + 2, :] for s in range(NX))
+            total = sum(w[s] * stat_all[s, rows_of[k], 2 * head + 1:2 * head + 2, :] for s in range(NX))
             rows = slice(head * HEAD, (head + 1) * HEAD)
             share = 1.0 / total
-            value = sum(o_all[s, i, rows, :].astype(jnp.float32) * (w[s] * share) for s in range(NX))
-            result[i, :, rows] = value.T.astype(jnp.bfloat16)
-        if i:
-            ship(i - 1)
+            value = sum(o_all[s, k, rows, :].astype(jnp.float32) * (w[s] * share) for s in range(NX))
+            result[k, :, rows] = value.T.astype(jnp.bfloat16)
+        if k:
+            ship(k - 1)
     ship(3)
 
     for zs in range(NZ):
@@ -504,15 +511,8 @@
         @pl.when(jnp.logical_not(local))
         def _(zs=zs):
             waiter(out.at[:, columns(zs)], z_recv.at[zs]).wait_recv()
-    for i in range(4):
-        for cc in range(2):
-            @pl.when(is_local(i, cc))
-            def _():
-                local_of(i, cc).wait()
-
-            @pl.when(jnp.logical_not(is_local(i, cc)))
-            def _():
-                remote_of(i, cc).wait_send()
+    for k in range(4):
+        deliver(k, lambda copy: copy.wait(), lambda copy: copy.wait_send())
     for copy in sends:
         copy.wait_send()
 
@@ -530,7 +530,7 @@
             pltpu.VMEM((NX, 4, 8, BLOCK), jnp.float32),
             pltpu.VMEM((4, BLOCK, SLAB), jnp.bfloat16),
             dma((NX, 4)), dma((NX, 4)), dma((NX,)), dma((NX,)),
-            dma((4, 2)), dma((NZ,)), dma((3,)),
+            dma((4, 2)), dma((NZ,)), dma((6,)),
         ],
         compiler_params=pltpu.CompilerParams(
             collective_id=1, has_side_effects=True, vmem_limit_bytes=8 * 1024 * 1024),

time: 118 us -> 115 us (0.975)
  Pallas kernels: 117 us -> 114 us
  other arithmetic: 1.35 us -> 0 us
    pallas_call x1, Pallas kernels: 35.4 us -> 33.1 us  [merge(): pl.pallas_call(merge_kernel, out_shape=jax.ShapeDtypeStruct((HALF, NZ * S...]
    concatenate x1 -> x0, other arithmetic: 1.35 us -> none  [gather(): jnp.concatenate((queries, keys, values), axis=0)]
where the time goes in v5:
time: 115 us
  Pallas kernels  114 us (99%)
    pallas_call x1, Pallas kernels, gather(): pl.pallas_call(gather_kernel, out_shape=(jax.ShapeDtypeStruct((NY, NZ, 2,...  46.6 us
    pallas_call x1, Pallas kernels, attend(): pl.pallas_call(attend_kernel, out_shape=(jax.ShapeDtypeStruct((ITEMS + 1,...  34.1 us
    pallas_call x1, Pallas kernels, merge(): pl.pallas_call(merge_kernel, out_shape=jax.ShapeDtypeStruct((HALF, NZ * S...  33.1 us

profile of v5, /device:TPU:25, one launch (start us, length us, event | category | flops | bytes accessed | tf_op | source)
XLA Modules:
  0.0 114.6 jit_solution(14373646019155350236)
XLA Ops:
  0.0 46.6 %gather.1 = (bf16[4,8,2,64,768]{4,3,2,1,0:T(8,128)(2,1)S(1)}, bf16[4,4,2,64,384]{4,3,2,1,0:T(8,128)(2,1)S(1)}, s32[56,128]{1,0:T(8,128)S(1)}) custom-call(bf16[64,3072]{1,0:T(8,128)(2,1)} %q_in.1, bf16[64,3072]{1,0:T(8,128)(2,1)} %k_in.1, bf16[64,3072]{1,0:T(8,128)(2,1)} %v_in.1, s32[3,128,128]{2,1,0:T(8,128)} %mask_in.1, s32[1,128]{1,0:T(1,128)} %bitcast.5), custom_call_target="tpu_custom_call" | custom-call | tf_op jit(solution)/shard_map/gather/pallas_call | solution.py:267
  46.6 34.1 %attend.1 = (bf16[17,384,128]{2,1,0:T(8,128)(2,1)S(1)}, f32[17,8,128]{2,1,0:T(8,128)S(1)}) custom-call(s32[56,128]{1,0:T(8,128)S(1)} %get-tuple-element.10.lists, bf16[32,128,768]{2,1,0:T(8,128)(2,1)S(1)} %bitcast.3, bf16[16,128,384]{2,1,0:T(8,128)(2,1)S(1)} %bitcast.4), custom_call_target="tpu_custom_call" | custom-call | tf_op jit(solution)/shard_map/attend/pallas_call | solution.py:398
  80.8 33.1 %merge.1 = bf16[64,3072]{1,0:T(8,128)(2,1)S(1)} custom-call(bf16[17,384,128]{2,1,0:T(8,128)(2,1)S(1)} %get-tuple-element.13.o_in, f32[17,8,128]{2,1,0:T(8,128)S(1)} %get-tuple-element.14.stat_in), custom_call_target="tpu_custom_call" | custom-call | tf_op jit(solution)/shard_map/merge/pallas_call | solution.py:523
  113.8 0.7 copy.7

commit v6 on v5

--- a/solution.py
+++ b/solution.py
@@ -17,7 +17,7 @@
 KBLOCKS = NY * NZ
 LIST_ROWS = HEADS_HERE * ITEMS + 8
 UNROLL = 4
-WIDE = 2
+WIDE = 6
 NEG = -1e30
 BIG = 1e30
 COEF = math.log2(math.e) / math.sqrt(HEAD)

time: 115 us -> 109 us (0.948)
  Pallas kernels: 114 us -> 108 us
    pallas_call x1, Pallas kernels: 34.1 us -> 30.2 us  [attend(): pl.pallas_call(attend_kernel, out_shape=(jax.ShapeDtypeStruct((ITEMS + 1,...]
    pallas_call x1, Pallas kernels: 33.1 us -> 31.4 us  [merge(): pl.pallas_call(merge_kernel, out_shape=jax.ShapeDtypeStruct((HALF, NZ * S...]
where the time goes in v6:
time: 109 us
  Pallas kernels  108 us (99%)
    pallas_call x1, Pallas kernels, gather(): pl.pallas_call(gather_kernel, out_shape=(jax.ShapeDtypeStruct((NY, NZ, 2,...  46.6 us
    pallas_call x1, Pallas kernels, merge(): pl.pallas_call(merge_kernel, out_shape=jax.ShapeDtypeStruct((HALF, NZ * S...  31.4 us
    pallas_call x1, Pallas kernels, attend(): pl.pallas_call(attend_kernel, out_shape=(jax.ShapeDtypeStruct((ITEMS + 1,...  30.2 us

profile of v6, /device:TPU:25, one launch (start us, length us, event | category | flops | bytes accessed | tf_op | source)
XLA Modules:
  0.0 109.0 jit_solution(4992968120406683942)
XLA Ops:
  0.0 46.6 %gather.1 = (bf16[4,8,2,64,768]{4,3,2,1,0:T(8,128)(2,1)S(1)}, bf16[4,4,2,64,384]{4,3,2,1,0:T(8,128)(2,1)S(1)}, s32[56,128]{1,0:T(8,128)S(1)}) custom-call(bf16[64,3072]{1,0:T(8,128)(2,1)} %q_in.1, bf16[64,3072]{1,0:T(8,128)(2,1)} %k_in.1, bf16[64,3072]{1,0:T(8,128)(2,1)} %v_in.1, s32[3,128,128]{2,1,0:T(8,128)} %mask_in.1, s32[1,128]{1,0:T(1,128)} %bitcast.5), custom_call_target="tpu_custom_call" | custom-call | tf_op jit(solution)/shard_map/gather/pallas_call | solution.py:267
  46.6 30.2 %attend.1 = (bf16[17,384,128]{2,1,0:T(8,128)(2,1)S(1)}, f32[17,8,128]{2,1,0:T(8,128)S(1)}) custom-call(s32[56,128]{1,0:T(8,128)S(1)} %get-tuple-element.10.lists, bf16[32,128,768]{2,1,0:T(8,128)(2,1)S(1)} %bitcast.3, bf16[16,128,384]{2,1,0:T(8,128)(2,1)S(1)} %bitcast.4), custom_call_target="tpu_custom_call" | custom-call | tf_op jit(solution)/shard_map/attend/pallas_call | solution.py:398
  76.9 31.4 %merge.1 = bf16[64,3072]{1,0:T(8,128)(2,1)S(1)} custom-call(bf16[17,384,128]{2,1,0:T(8,128)(2,1)S(1)} %get-tuple-element.13.o_in, f32[17,8,128]{2,1,0:T(8,128)S(1)} %get-tuple-element.14.stat_in), custom_call_target="tpu_custom_call" | custom-call | tf_op jit(solution)/shard_map/merge/pallas_call | solution.py:523
  108.2 0.7 copy.7
